TPU v7x, 32 devices: a whole 2x2x4 slice. The times are simulated.
32 devices in a mesh: ctx: 16 (over z, y, x), tp: 2 (over core).
Axes of the slice: x: 2, y: 2, z: 4, core: 2. Of those that a mesh axis runs over, the one named last changes fastest.
Arguments:
- queries: bfloat16 [4096, 8192], P('ctx', 'tp'), may hold values from -8 to 8
- span_kv: bfloat16 [4096, 8, 2, 128], P('ctx', 'tp'), may hold values from -8 to 8
- cache_kv: bfloat16 [8192, 8, 2, 128], P('ctx', 'tp'), may hold values from -4 to 4
- out_weight: bfloat16 [8192, 8192], P('tp', 'ctx'), may hold values from -2.390625 to 2.390625
- offset: int32 [1], replicated, may hold values from 8192 to 16383
- lengths: int32 [32], replicated, may hold values from 64 to 256, as said below
Outputs:
- mixed: bfloat16 [4096, 8192], P('tp', 'ctx')
Inputs may be any that keep to these rules, and one draw needn't show every extreme that they name: `lengths`: each at most 256; in every draw some match has all 256 of its positions valid.
All inputs are finite; a program needn't handle non-finite values.
Results may differ from a plain program's by a relative error of at most 0.025.
Values may be sent and summed in bfloat16 or wider, within the bound.
No kernel may reach another device: no remote copies, remote signals or barrier semaphores. Data moves between devices by JAX's collectives and lax.ppermute only.
A program may use at most 192 MiB of HBM per device.

v0:
```python
import math

import jax
import jax.numpy as jnp
from jax import lax
from jax.sharding import PartitionSpec as P

SLOT = 256


lowest_score = -1e30
rope_base = 500000.0


def rotate(values, positions):
    head_size = values.shape[-1]
    half_dim = head_size // 2
    frequency = jnp.exp(
        jnp.arange(half_dim, dtype=jnp.float32) * (-2.0 * math.log(rope_base) / head_size)
    )
    angles = positions.astype(jnp.float32)[:, None] * frequency[None, :]
    cosine = jnp.cos(angles)[:, None, :]
    sine_part = jnp.sin(angles)[:, None, :]
    first_half = values[..., :half_dim]
    second_half = values[..., half_dim:]
    return jnp.concatenate(
        [
            first_half * cosine - second_half * sine_part,
            second_half * cosine + first_half * sine_part,
        ],
        axis=-1,
    )


def key_block(count):
    for option in (2048, 1536, 1024, 768, 512, 384, 256, 128):
        return option
    return count


def slot_valid(cache_positions, lengths):
    match_ids = jnp.arange(lengths.shape[0], dtype=jnp.int32)
    owner = cache_positions // SLOT
    limit = jnp.sum(jnp.where(owner[:, None] == match_ids[None, :], lengths[None, :], 0), axis=1)
    return cache_positions % SLOT < limit


def online_update(carry_state, grouped, key_rows, value_rows, valid, scale):
    running_max, running_sum, accum = carry_state
    scores = (
        jnp.einsum("tkgd,nkd->tkgn", grouped, key_rows, preferred_element_type=jnp.float32) * scale
    )
    scores = jnp.where(valid, scores, lowest_score)
    new_max = jnp.maximum(running_max, jnp.max(scores, axis=-1))
    factor = jnp.exp(running_max - new_max)
    weights = jnp.where(valid, jnp.exp(scores - new_max[..., None]), 0.0)
    running_sum = running_sum * factor + jnp.sum(weights, axis=-1)
    update = jnp.einsum(
        "tkgn,nkd->tkgd",
        weights.astype(jnp.bfloat16),
        value_rows,
        preferred_element_type=jnp.float32,
    )
    accum = accum * factor[..., None] + update
    return (new_max, running_sum, accum)


def fold_blocks(carry_state, grouped, piece, mask_rule, scale):
    count = piece.shape[0]
    block = key_block(count)
    block_count = count // block
    kv_local = piece.shape[1]
    head_size = piece.shape[3]
    key_rows = piece[:, :, 0, :].reshape(block_count, block, kv_local, head_size)
    value_rows = piece[:, :, 1, :].reshape(block_count, block, kv_local, head_size)

    def advance(state_now, inputs):
        block_keys, block_values, index = inputs
        positions = index * block + jnp.arange(block, dtype=jnp.int32)
        valid = mask_rule(positions)
        return (online_update(state_now, grouped, block_keys, block_values, valid, scale), None)

    result, unused = lax.scan(
        advance, carry_state, (key_rows, value_rows, jnp.arange(block_count, dtype=jnp.int32))
    )
    return result


def body(queries, span_kv, cache_kv, out_weight, offset, lengths):
    tok_rows, width = queries.shape
    kv_local = span_kv.shape[1]
    head_size = span_kv.shape[3]
    heads_local = width // head_size
    group = heads_local // kv_local
    cache_rows = cache_kv.shape[0]
    scale = 1.0 / math.sqrt(head_size)
    ctx_index = lax.axis_index("ctx")
    first_token = ctx_index * tok_rows
    token_ids = first_token + jnp.arange(tok_rows, dtype=jnp.int32)
    positions = offset[0] + token_ids
    rotated = rotate(
        queries.reshape(tok_rows, heads_local, head_size).astype(jnp.float32), positions
    ).astype(jnp.bfloat16)
    grouped = rotated.reshape(tok_rows, kv_local, group, head_size)
    span_keys = rotate(span_kv[:, :, 0, :].astype(jnp.float32), positions).astype(jnp.bfloat16)
    span_rotated = jnp.stack([span_keys, span_kv[:, :, 1, :]], axis=2)

    def joint_rule(key_positions):
        stride = cache_rows + tok_rows
        shard = key_positions // stride
        within = key_positions % stride
        in_cache = within < cache_rows
        cache_positions = shard * cache_rows + jnp.minimum(within, cache_rows - 1)
        span_positions = shard * tok_rows + within - cache_rows
        from_cache = slot_valid(cache_positions, lengths)[None, :]
        from_span = span_positions[None, :] <= token_ids[:, None]
        return jnp.where(in_cache[None, :], from_cache, from_span)[:, None, None, :]

    start_state = (
        jnp.full((tok_rows, kv_local, group), lowest_score, jnp.float32),
        jnp.zeros((tok_rows, kv_local, group), jnp.float32),
        jnp.zeros((tok_rows, kv_local, group, head_size), jnp.float32),
    )
    local_entries = jnp.concatenate([cache_kv, span_rotated], axis=0)
    state_now = fold_blocks(
        start_state,
        grouped,
        lax.all_gather(local_entries, "ctx", axis=0, tiled=True),
        joint_rule,
        scale,
    )
    attention = (state_now[2] / state_now[1][..., None]).astype(jnp.bfloat16)
    attention = attention.reshape(tok_rows, heads_local * head_size)
    projected = jnp.dot(
        lax.all_gather(attention, "ctx", axis=0, tiled=True),
        out_weight,
        preferred_element_type=jnp.float32,
    )
    return lax.psum_scatter(projected.astype(jnp.bfloat16), "tp", scatter_dimension=0, tiled=True)


def solution(mesh):
    return jax.shard_map(
        body,
        mesh=mesh,
        in_specs=(
            P("ctx", "tp"),
            P("ctx", "tp", None, None),
            P("ctx", "tp", None, None),
            P("tp", "ctx"),
            P(),
            P(),
        ),
        out_specs=P("tp", "ctx"),
        check_vma=False,
    )
```

profile of v0, /device:TPU:0, one launch (start us, length us, event | category | flops | bytes accessed | tf_op | source)
XLA Modules:
  0.0 1502.3 jit_solution(11750166984928818352)
XLA Ops:
  7.2 2.1 fusion.34
  9.3 0.5 copy.39
  9.9 0.5 copy.40
  10.4 0.3 multiply_cosine_fusion
  11.1 1.5 copy.26
  12.6 1.2 pad_maximum_fusion.1
  14.2 0.5 convert_bitcast_fusion
  14.6 2.7 copy.43
  17.4 4.9 fusion.33
  22.3 4.9 subtract_convert_fusion
  27.2 1.2 pad_maximum_fusion
  28.4 258.9 %all-gather.3.cloned.1.call-done = bf16[12288,4,2,128]{3,0,1,2:T(8,128)(2,1)} async-done(((bf16[768,4,2,128]{3,0,1,2:T(8,128)(2,1)}), bf16[12288,4,2,128]{3,0,1,2:T(8,128)(2,1)}) %all-gather.3.cloned.1.call-update) | async-done | bytes 25165840 | tf_op jit(solution)/shard_map/all_gather | solution.py:128
  287.3 18.1 %fusion.32 = (bf16[12288,4,1,128]{3,0,1,2:T(8,128)(2,1)}, bf16[12288,4,1,128]{3,0,1,2:T(8,128)(2,1)}) fusion(bf16[12288,4,2,128]{3,0,1,2:T(8,128)(2,1)} %all-gather.3.cloned.1.call-done), kind=kLoop, calls=%fused_computation.66 | loop fusion | bytes 50331648 | tf_op jit(solution)/shard_map/slice | solution.py:75
  305.4 465.5 %while.18 = (s32[]{:T(128)}, f32[256,4,8]{0,2,1:T(8,128)S(1)}, f32[256,4,8]{0,2,1:T(8,128)S(1)}, f32[256,4,8,128]{0,3,2,1:T(8,128)}, s32[6]{0:T(128)S(1)}, /*ind...) while((s32[]{:T(128)}, f32[256,4,8]{0,2,1:T(8,128)S(1)}, ...), condition=%wide.region_4.5_spmd.clone, body=%wide.region_0.4_spmd.clone.sunk | while | flops 8812611584 | bytes 218688816 | solution.py:83
  305.4 0.6 dynamic_slice.41
  306.9 1.7 compare_select_fusion.2
  308.6 24.9 %fusion.51 = (f32[256,4,8]{0,2,1:T(8,128)S(1)}, f32[4,2048,256,8]{2,1,3,0:T(8,128)}) fusion(pred[256,2048]{0,1:T(8,128)(4,1)S(1)} %compare_select_fusion.2, bf16[256,4,8,128]{3,0,2,1:T(8,128)(2,1)S(1)} %get-tuple-element.380, bf16[6,2048,4,128]{3,1,0,2:T(8,128)(2,1)} %get-tuple-element.379, s32[]{:T(128)} %get-tuple-element.360), kind=kOutput, calls=%fused_computation.3.clone.1 | convolution fusion | flops 4345290752 | bytes 71860736 | tf_op jit(solution)/shard_map/while/body/eval_jaxpr/tkgd,nkd->tkgn/dot_general | solution.py:51
  333.5 21.7 %fusion.52 = f32[256,4,8]{0,2,1:T(8,128)S(1)} fusion(f32[4,2048,256,8]{2,1,3,0:T(8,128)} %get-tuple-element.344, f32[256,4,8]{0,2,1:T(8,128)S(1)} %select_maximum_fusion.2, pred[256,2048]{0,1:T(8,128)(4,1)S(1)} %compare_select_fusion.2), kind=kLoop, calls=%fused_computation.5.clone.1 | loop fusion | flops 83877888 | bytes 67698688 | tf_op jit(solution)/shard_map/while/body/eval_jaxpr/reduce_sum | solution.py:57
  355.3 26.9 %bitcast_add_fusion.2 = f32[256,4,8,128]{0,3,2,1:T(8,128)} fusion(f32[256,4,8,128]{0,3,2,1:T(8,128)} %get-tuple-element.363, f32[4,2048,256,8]{2,1,3,0:T(8,128)} %get-tuple-element.344, f32[256,4,8]{0,2,1:T(8,128)S(1)} %select_maximum_fusion.2, pred[256,2048]{0,1:T(8,128)(4,1)S(1)} %compare_select_fusion.2, ...), kind=kOutput, calls=%fused_computation.8.clone.1 | convolution fusion | flops 4381999104 | bytes 78184960 | tf_op jit(solution)/shard_map/while/body/eval_jaxpr/tkgn,nkd->tkgd/dot_general | solution.py:58
  382.1 0.6 dynamic_slice.41
  383.6 1.7 compare_select_fusion.2
  385.3 24.9 %fusion.51 = (f32[256,4,8]{0,2,1:T(8,128)S(1)}, f32[4,2048,256,8]{2,1,3,0:T(8,128)}) fusion(pred[256,2048]{0,1:T(8,128)(4,1)S(1)} %compare_select_fusion.2, bf16[256,4,8,128]{3,0,2,1:T(8,128)(2,1)S(1)} %get-tuple-element.380, bf16[6,2048,4,128]{3,1,0,2:T(8,128)(2,1)} %get-tuple-element.379, s32[]{:T(128)} %get-tuple-element.360), kind=kOutput, calls=%fused_computation.3.clone.1 | convolution fusion | flops 4345290752 | bytes 71860736 | tf_op jit(solution)/shard_map/while/body/eval_jaxpr/tkgd,nkd->tkgn/dot_general | solution.py:51
  410.2 21.7 %fusion.52 = f32[256,4,8]{0,2,1:T(8,128)S(1)} fusion(f32[4,2048,256,8]{2,1,3,0:T(8,128)} %get-tuple-element.344, f32[256,4,8]{0,2,1:T(8,128)S(1)} %select_maximum_fusion.2, pred[256,2048]{0,1:T(8,128)(4,1)S(1)} %compare_select_fusion.2), kind=kLoop, calls=%fused_computation.5.clone.1 | loop fusion | flops 83877888 | bytes 67698688 | tf_op jit(solution)/shard_map/while/body/eval_jaxpr/reduce_sum | solution.py:57
  432.0 27.9 %bitcast_add_fusion.2 = f32[256,4,8,128]{0,3,2,1:T(8,128)} fusion(f32[256,4,8,128]{0,3,2,1:T(8,128)} %get-tuple-element.363, f32[4,2048,256,8]{2,1,3,0:T(8,128)} %get-tuple-element.344, f32[256,4,8]{0,2,1:T(8,128)S(1)} %select_maximum_fusion.2, pred[256,2048]{0,1:T(8,128)(4,1)S(1)} %compare_select_fusion.2, ...), kind=kOutput, calls=%fused_computation.8.clone.1 | convolution fusion | flops 4381999104 | bytes 78184960 | tf_op jit(solution)/shard_map/while/body/eval_jaxpr/tkgn,nkd->tkgd/dot_general | solution.py:58
  459.9 0.6 dynamic_slice.41
  461.3 1.7 compare_select_fusion.2
  463.1 24.9 %fusion.51 = (f32[256,4,8]{0,2,1:T(8,128)S(1)}, f32[4,2048,256,8]{2,1,3,0:T(8,128)}) fusion(pred[256,2048]{0,1:T(8,128)(4,1)S(1)} %compare_select_fusion.2, bf16[256,4,8,128]{3,0,2,1:T(8,128)(2,1)S(1)} %get-tuple-element.380, bf16[6,2048,4,128]{3,1,0,2:T(8,128)(2,1)} %get-tuple-element.379, s32[]{:T(128)} %get-tuple-element.360), kind=kOutput, calls=%fused_computation.3.clone.1 | convolution fusion | flops 4345290752 | bytes 71860736 | tf_op jit(solution)/shard_map/while/body/eval_jaxpr/tkgd,nkd->tkgn/dot_general | solution.py:51
  488.0 21.7 %fusion.52 = f32[256,4,8]{0,2,1:T(8,128)S(1)} fusion(f32[4,2048,256,8]{2,1,3,0:T(8,128)} %get-tuple-element.344, f32[256,4,8]{0,2,1:T(8,128)S(1)} %select_maximum_fusion.2, pred[256,2048]{0,1:T(8,128)(4,1)S(1)} %compare_select_fusion.2), kind=kLoop, calls=%fused_computation.5.clone.1 | loop fusion | flops 83877888 | bytes 67698688 | tf_op jit(solution)/shard_map/while/body/eval_jaxpr/reduce_sum | solution.py:57
  509.7 27.9 %bitcast_add_fusion.2 = f32[256,4,8,128]{0,3,2,1:T(8,128)} fusion(f32[256,4,8,128]{0,3,2,1:T(8,128)} %get-tuple-element.363, f32[4,2048,256,8]{2,1,3,0:T(8,128)} %get-tuple-element.344, f32[256,4,8]{0,2,1:T(8,128)S(1)} %select_maximum_fusion.2, pred[256,2048]{0,1:T(8,128)(4,1)S(1)} %compare_select_fusion.2, ...), kind=kOutput, calls=%fused_computation.8.clone.1 | convolution fusion | flops 4381999104 | bytes 78184960 | tf_op jit(solution)/shard_map/while/body/eval_jaxpr/tkgn,nkd->tkgd/dot_general | solution.py:58
  537.7 0.6 dynamic_slice.41
  539.1 1.7 compare_select_fusion.2
  540.8 24.9 %fusion.51 = (f32[256,4,8]{0,2,1:T(8,128)S(1)}, f32[4,2048,256,8]{2,1,3,0:T(8,128)}) fusion(pred[256,2048]{0,1:T(8,128)(4,1)S(1)} %compare_select_fusion.2, bf16[256,4,8,128]{3,0,2,1:T(8,128)(2,1)S(1)} %get-tuple-element.380, bf16[6,2048,4,128]{3,1,0,2:T(8,128)(2,1)} %get-tuple-element.379, s32[]{:T(128)} %get-tuple-element.360), kind=kOutput, calls=%fused_computation.3.clone.1 | convolution fusion | flops 4345290752 | bytes 71860736 | tf_op jit(solution)/shard_map/while/body/eval_jaxpr/tkgd,nkd->tkgn/dot_general | solution.py:51
  565.7 21.7 %fusion.52 = f32[256,4,8]{0,2,1:T(8,128)S(1)} fusion(f32[4,2048,256,8]{2,1,3,0:T(8,128)} %get-tuple-element.344, f32[256,4,8]{0,2,1:T(8,128)S(1)} %select_maximum_fusion.2, pred[256,2048]{0,1:T(8,128)(4,1)S(1)} %compare_select_fusion.2), kind=kLoop, calls=%fused_computation.5.clone.1 | loop fusion | flops 83877888 | bytes 67698688 | tf_op jit(solution)/shard_map/while/body/eval_jaxpr/reduce_sum | solution.py:57
  587.5 27.9 %bitcast_add_fusion.2 = f32[256,4,8,128]{0,3,2,1:T(8,128)} fusion(f32[256,4,8,128]{0,3,2,1:T(8,128)} %get-tuple-element.363, f32[4,2048,256,8]{2,1,3,0:T(8,128)} %get-tuple-element.344, f32[256,4,8]{0,2,1:T(8,128)S(1)} %select_maximum_fusion.2, pred[256,2048]{0,1:T(8,128)(4,1)S(1)} %compare_select_fusion.2, ...), kind=kOutput, calls=%fused_computation.8.clone.1 | convolution fusion | flops 4381999104 | bytes 78184960 | tf_op jit(solution)/shard_map/while/body/eval_jaxpr/tkgn,nkd->tkgd/dot_general | solution.py:58
  615.4 0.6 dynamic_slice.41
  616.9 1.7 compare_select_fusion.2
  618.6 24.9 %fusion.51 = (f32[256,4,8]{0,2,1:T(8,128)S(1)}, f32[4,2048,256,8]{2,1,3,0:T(8,128)}) fusion(pred[256,2048]{0,1:T(8,128)(4,1)S(1)} %compare_select_fusion.2, bf16[256,4,8,128]{3,0,2,1:T(8,128)(2,1)S(1)} %get-tuple-element.380, bf16[6,2048,4,128]{3,1,0,2:T(8,128)(2,1)} %get-tuple-element.379, s32[]{:T(128)} %get-tuple-element.360), kind=kOutput, calls=%fused_computation.3.clone.1 | convolution fusion | flops 4345290752 | bytes 71860736 | tf_op jit(solution)/shard_map/while/body/eval_jaxpr/tkgd,nkd->tkgn/dot_general | solution.py:51
  643.5 21.7 %fusion.52 = f32[256,4,8]{0,2,1:T(8,128)S(1)} fusion(f32[4,2048,256,8]{2,1,3,0:T(8,128)} %get-tuple-element.344, f32[256,4,8]{0,2,1:T(8,128)S(1)} %select_maximum_fusion.2, pred[256,2048]{0,1:T(8,128)(4,1)S(1)} %compare_select_fusion.2), kind=kLoop, calls=%fused_computation.5.clone.1 | loop fusion | flops 83877888 | bytes 67698688 | tf_op jit(solution)/shard_map/while/body/eval_jaxpr/reduce_sum | solution.py:57
  665.3 27.9 %bitcast_add_fusion.2 = f32[256,4,8,128]{0,3,2,1:T(8,128)} fusion(f32[256,4,8,128]{0,3,2,1:T(8,128)} %get-tuple-element.363, f32[4,2048,256,8]{2,1,3,0:T(8,128)} %get-tuple-element.344, f32[256,4,8]{0,2,1:T(8,128)S(1)} %select_maximum_fusion.2, pred[256,2048]{0,1:T(8,128)(4,1)S(1)} %compare_select_fusion.2, ...), kind=kOutput, calls=%fused_computation.8.clone.1 | convolution fusion | flops 4381999104 | bytes 78184960 | tf_op jit(solution)/shard_map/while/body/eval_jaxpr/tkgn,nkd->tkgd/dot_general | solution.py:58
  693.2 0.6 dynamic_slice.41
  694.6 1.7 compare_select_fusion.2
  696.4 24.9 %fusion.51 = (f32[256,4,8]{0,2,1:T(8,128)S(1)}, f32[4,2048,256,8]{2,1,3,0:T(8,128)}) fusion(pred[256,2048]{0,1:T(8,128)(4,1)S(1)} %compare_select_fusion.2, bf16[256,4,8,128]{3,0,2,1:T(8,128)(2,1)S(1)} %get-tuple-element.380, bf16[6,2048,4,128]{3,1,0,2:T(8,128)(2,1)} %get-tuple-element.379, s32[]{:T(128)} %get-tuple-element.360), kind=kOutput, calls=%fused_computation.3.clone.1 | convolution fusion | flops 4345290752 | bytes 71860736 | tf_op jit(solution)/shard_map/while/body/eval_jaxpr/tkgd,nkd->tkgn/dot_general | solution.py:51
  721.3 21.7 %fusion.52 = f32[256,4,8]{0,2,1:T(8,128)S(1)} fusion(f32[4,2048,256,8]{2,1,3,0:T(8,128)} %get-tuple-element.344, f32[256,4,8]{0,2,1:T(8,128)S(1)} %select_maximum_fusion.2, pred[256,2048]{0,1:T(8,128)(4,1)S(1)} %compare_select_fusion.2), kind=kLoop, calls=%fused_computation.5.clone.1 | loop fusion | flops 83877888 | bytes 67698688 | tf_op jit(solution)/shard_map/while/body/eval_jaxpr/reduce_sum | solution.py:57
  743.0 27.9 %bitcast_add_fusion.2 = f32[256,4,8,128]{0,3,2,1:T(8,128)} fusion(f32[256,4,8,128]{0,3,2,1:T(8,128)} %get-tuple-element.363, f32[4,2048,256,8]{2,1,3,0:T(8,128)} %get-tuple-element.344, f32[256,4,8]{0,2,1:T(8,128)S(1)} %select_maximum_fusion.2, pred[256,2048]{0,1:T(8,128)(4,1)S(1)} %compare_select_fusion.2, ...), kind=kOutput, calls=%fused_computation.8.clone.1 | convolution fusion | flops 4381999104 | bytes 78184960 | tf_op jit(solution)/shard_map/while/body/eval_jaxpr/tkgn,nkd->tkgd/dot_general | solution.py:58
  771.0 4.0 divide_convert_fusion
  775.1 682.2 %all-gather.5.cloned.1.call-done = bf16[4096,4096]{0,1:T(8,128)(2,1)} async-done(((bf16[256,4096]{0,1:T(8,128)(2,1)}), bf16[4096,4096]{0,1:T(8,128)(2,1)}) %all-gather.5.cloned.1.call-update) | async-done | bytes 33554448 | tf_op jit(solution)/shard_map/all_gather | solution.py:135
  1457.2 25.1 %convolution_convert_fusion = bf16[4096,512]{1,0:T(8,128)(2,1)} fusion(bf16[4096,4096]{0,1:T(8,128)(2,1)} %all-gather.5.cloned.1.call-done, bf16[4096,512]{1,0:T(8,128)(2,1)} %param.11), kind=kOutput, calls=%fused_computation.49 | convolution fusion | flops 17181966336 | bytes 41943040 | tf_op jit(solution)/shard_map/dot_general | solution.py:134
  1482.4 13.4 reduce-scatter.2.cloned.1.call-done
  (70 shorter events, 2.1 us)
Async XLA Ops:
  6.5 280.7 %all-gather.3.cloned.1.call-start = ((), (), s32[]{:S(2)}) async-start(), calls=%async_computation.1 | async-start | bytes 26738688 | tf_op jit(solution)/shard_map/all_gather | solution.py:128
  10.8 3.4 copy-start
  13.9 1443.3 %all-gather.5.cloned.1.call-start = ((), (), s32[]{:S(2)}) async-start(), calls=%async_computation.2 | async-start | bytes 35651584 | tf_op jit(solution)/shard_map/all_gather | solution.py:135
  28.4 277.1 %copy-start.1 = (s32[32]{0:T(128)S(1)}, s32[32]{0:T(128)}, u32[]{:S(2)}) copy-start(s32[32]{0:T(128)} %param.13) | copy-start | bytes 388
  775.0 720.8 %reduce-scatter.2.cloned.1.call-start = ((), (), s32[]{:S(2)}) async-start(), calls=%async_computation.3 | async-start | bytes 6291456 | tf_op jit(solution)/shard_map/reduce_scatter | solution.py:139
Sparse Core Ops, SparseCore 0:
  14.0 273.2 all-gather.2
  775.1 682.0 all-gather.4
  1482.5 13.2 reduce-scatter.1
where the time goes:
time: 1500 us
  waiting for transfers between devices  955 us (64%)
  matrix products  341 us (23%)
  other arithmetic  154 us (10%)
  local copies, waits for them, and re-layouts  34.3 us (2%)
    all_gather x1, waiting for transfers between devices, body(): lax.all_gather(attention, 'ctx', axis=0, tiled=True)  682 us
    all_gather x1, waiting for transfers between devices, body(): lax.all_gather(local_entries, 'ctx', axis=0, tiled=True)  259 us
    dot_general x6, matrix products, online_update(): jnp.einsum('tkgn,nkd->tkgd', weights.astype(jnp.bfloat16), value_rows, pr...  166 us
    dot_general x6, matrix products, online_update(): jnp.einsum('tkgd,nkd->tkgn', grouped, key_rows, preferred_element_type=jn...  149 us
    reduce_sum x6, other arithmetic, online_update(): running_sum = running_sum * factor + jnp.sum(weights, axis=-1)  130 us
  transfers between devices with their start and end apart: 3, of which 3 were waited for; matrix products, arithmetic and copies ran while one was open for 1% of the time, Pallas kernels for 0%

commit v1 on v0

v1 whole, which is shorter than its diff:
```python
import functools
import math

import jax
import jax.numpy as jnp
from jax import lax
from jax.experimental import pallas as pl
from jax.experimental.pallas import tpu as pltpu
from jax.sharding import Mesh
from jax.sharding import PartitionSpec as P


F32 = jnp.float32
BF16 = jnp.bfloat16
lowest_score = -1e30
rope_base = 500000.0
bound_limit = 90.0
key_rows = 512


def rotate(values, positions):
    head_size = values.shape[-1]
    half_dim = head_size // 2
    frequency = jnp.exp(
        jnp.arange(half_dim, dtype=F32) * (-2.0 * math.log(rope_base) / head_size)
    )
    angles = positions.astype(F32)[:, None] * frequency[None, :]
    cosine = jnp.cos(angles)[:, None, :]
    sine_part = jnp.sin(angles)[:, None, :]
    first_half = values[..., :half_dim]
    second_half = values[..., half_dim:]
    return jnp.concatenate(
        [
            first_half * cosine - second_half * sine_part,
            second_half * cosine + first_half * sine_part,
        ],
        axis=-1,
    )


def square_bound(rows):
    squares = (rows * rows).astype(BF16)
    ones = jnp.ones((rows.shape[1], rows.shape[1]), BF16)
    sums = jnp.dot(squares, ones, preferred_element_type=F32)
    return jnp.max(sums, axis=0, keepdims=True)


def attend(queries, entries, lengths, j, start, stride):
    chunks, rows, width = queries.shape
    count = chunks // stride
    nj, nz, local, pair = entries.shape
    head = pair // 2
    group = width // head
    cached = local - rows
    shards = nj * nz
    slots = lengths.shape[0]
    slot = cached * shards // slots
    per_shard = cached // slot
    span = shards * rows
    block = key_rows
    span_blocks = span // block
    stack = group * rows
    scale = math.log2(math.e) / math.sqrt(head)
    capacity = span + shards * cached + block

    def kernel(meta_ref, len_ref, q_ref, kv_ref, o_ref, keys, values, stacked, acc, top, norms, counts, bounds):
        step = pl.program_id(0)

        @pl.when(step == 0)
        def _():
            norms[...] = jnp.zeros_like(norms)

            def put_span(shard, carry):
                place = pl.ds(pl.multiple_of(shard * rows, rows), rows)
                piece = kv_ref[shard % nj, shard // nj, pl.ds(cached, rows), :]
                keys[place, :] = piece[:, :head]
                values[place, :head] = piece[:, head:]
                values[place, head:] = jnp.ones((rows, head), BF16)
                norms[...] = jnp.maximum(norms[...], square_bound(piece[:, :head].astype(F32)))
                return carry

            lax.fori_loop(0, shards, put_span, 0)
            index = lax.broadcasted_iota(jnp.int32, (slot, head), 0)

            def put_slot(number, at):
                shard = number // per_shard
                inside = pl.multiple_of((number % per_shard) * slot, slot)
                piece = kv_ref[shard % nj, shard // nj, pl.ds(inside, slot), :].astype(F32)
                size = len_ref[number]
                valid = index < size
                fixed = jnp.where(valid, piece[:, :head], piece[0:1, :head])
                place = pl.ds(pl.multiple_of(at, 16), slot)
                keys[place, :] = fixed.astype(BF16)
                values[place, :head] = jnp.where(valid, piece[:, head:], 0.0).astype(BF16)
                values[place, head:] = jnp.where(valid, 1.0, 0.0).astype(BF16)
                norms[...] = jnp.maximum(norms[...], square_bound(fixed))
                return at + (size + 15) // 16 * 16

            end = lax.fori_loop(0, slots, put_slot, span)
            place = pl.ds(pl.multiple_of(end, 16), block)
            keys[place, :] = jnp.broadcast_to(kv_ref[0, 0, 0:1, :head], (block, head))
            values[place, :] = jnp.zeros((block, pair), BF16)
            counts[0] = (end - span + block - 1) // block
            bounds[0] = jnp.max(norms[...])

        for g in range(group):
            stacked[g * rows : (g + 1) * rows, :] = q_ref[0, :, g * head : (g + 1) * head]
        acc[...] = jnp.zeros_like(acc)
        first_token = (meta_ref[0] + (meta_ref[1] + step * stride) * nj) * rows
        full = first_token // block
        total = full + counts[0]
        query_bound = jnp.max(square_bound(stacked[...].astype(F32)))
        safe = query_bound * bounds[0] * (1.05 * scale * scale) <= bound_limit * bound_limit

        def scores_of(at):
            raw = lax.dot_general(
                stacked[...],
                keys[pl.ds(at, block), :],
                (((1,), (1,)), ((), ())),
                preferred_element_type=F32,
            )
            return raw * scale

        token = first_token + lax.broadcasted_iota(jnp.int32, (stack, block), 0) % rows
        column = lax.broadcasted_iota(jnp.int32, (stack, block), 1)

        def place_of(i):
            return pl.multiple_of(jnp.where(i < full, i, span_blocks + i - full) * block, block)

        def add_plain(at, scores):
            weights = jnp.exp2(scores).astype(BF16)
            acc[...] += jnp.dot(weights, values[pl.ds(at, block), :], preferred_element_type=F32)

        @pl.when(safe)
        def _():
            def body(i, carry):
                at = place_of(i)
                add_plain(at, scores_of(at))
                return carry

            lax.fori_loop(0, total, body, 0)
            at = pl.multiple_of(full * block, block)
            add_plain(at, jnp.where(at + column <= token, scores_of(at), lowest_score))

        @pl.when(jnp.logical_not(safe))
        def _():
            top[...] = jnp.full_like(top, lowest_score)

            def body(i, carry):
                last = i == total
                at = jnp.where(last, pl.multiple_of(full * block, block), place_of(i))
                at = pl.multiple_of(at, block)
                entry = jnp.where(last, at, -block) + column
                scores = jnp.where(entry <= token, scores_of(at), lowest_score)
                before = top[...]
                now = jnp.maximum(before, jnp.max(scores, axis=1, keepdims=True))
                factor = jnp.exp2(before - now)
                weights = jnp.exp2(scores - now[:, :1]).astype(BF16)
                fresh = jnp.dot(weights, values[pl.ds(at, block), :], preferred_element_type=F32)
                acc[...] = acc[...] * jnp.concatenate([factor, factor], axis=1) + fresh
                top[...] = now
                return carry

            lax.fori_loop(0, total + 1, body, 0)

        for g in range(group):
            part = slice(g * rows, (g + 1) * rows)
            o_ref[0, :, g * head : (g + 1) * head] = (acc[part, :head] / acc[part, head:]).astype(BF16)

    grid_spec = pltpu.PrefetchScalarGridSpec(
        num_scalar_prefetch=2,
        grid=(count,),
        in_specs=[
            pl.BlockSpec((1, rows, width), lambda i, meta, size: (meta[1] + i * stride, 0, 0)),
            pl.BlockSpec(memory_space=pltpu.VMEM),
        ],
        out_specs=pl.BlockSpec((1, rows, width), lambda i, meta, size: (i, 0, 0)),
        scratch_shapes=[
            pltpu.VMEM((capacity, head), BF16),
            pltpu.VMEM((capacity, pair), BF16),
            pltpu.VMEM((stack, head), BF16),
            pltpu.VMEM((stack, pair), F32),
            pltpu.VMEM((stack, head), F32),
            pltpu.VMEM((1, head), F32),
            pltpu.SMEM((1,), jnp.int32),
            pltpu.SMEM((1,), F32),
        ],
    )
    return pl.pallas_call(
        kernel,
        grid_spec=grid_spec,
        out_shape=jax.ShapeDtypeStruct((count, rows, width), BF16),
        compiler_params=pltpu.CompilerParams(vmem_limit_bytes=60 << 20),
        name="attend",
    )(jnp.stack([j, jnp.int32(start)]).astype(jnp.int32), lengths, queries, entries)


def project(rotated, entries, lengths, out_weight, j, nz, nj, nt):
    groups = nz // nt
    rows, columns = rotated.shape[1], out_weight.shape[1]
    tp = lax.axis_index("tp")
    entries, out_weight = lax.optimization_barrier((entries, out_weight))
    swaps = [[(i, i ^ r) for i in range(nj)] for r in range(nj)]
    weights = [out_weight]
    for r in range(1, nj):
        weights.append(lax.ppermute(out_weight, "j", swaps[r]))
    wide = []
    for g in range(groups):
        part = attend(rotated, entries, lengths, j, g, groups)
        wide.append(lax.all_gather(part, "z", axis=2, tiled=True))
    out = jnp.zeros((groups, nj, rows, columns), BF16)
    ready = []
    for g in range(groups):
        wide[g], ready = lax.optimization_barrier((wide[g], ready))
        for r in [0] + list(range(1, nj)):
            partial = jnp.einsum("ctk,kn->ctn", wide[g], weights[r], preferred_element_type=F32)
            total = lax.dynamic_index_in_dim(partial, tp, 0, keepdims=False)
            for step in range(1, nt):
                turn = [(i, (i + step) % nt) for i in range(nt)]
                away = lax.dynamic_index_in_dim(partial, (tp + step) % nt, 0, keepdims=False)
                total = total + lax.ppermute(away.astype(BF16), "tp", turn).astype(F32)
            total = total.astype(BF16)
            ready.append(total[:1, :1])
            if r:
                total = lax.ppermute(total, "j", swaps[r])
            out = lax.dynamic_update_slice(out, total[None, None], (g, j ^ r, 0, 0))
    return out.reshape(groups * nj * rows, columns)


def body(queries, span_kv, cache_kv, out_weight, offset, lengths, *, nz, nj, nt):
    rows, width = queries.shape
    kv_local, head = span_kv.shape[1], span_kv.shape[3]
    cached = cache_kv.shape[0]
    z = lax.axis_index("z")
    j = lax.axis_index("j")
    positions = offset[0] + (z * nj + j) * rows + jnp.arange(rows, dtype=jnp.int32)

    span_keys = rotate(span_kv[:, :, 0, :].astype(F32), positions).astype(BF16)
    span_part = jnp.concatenate([span_keys, span_kv[:, :, 1, :]], axis=-1)
    cache_part = cache_kv.reshape(cached, kv_local, 2 * head)
    local = jnp.concatenate([cache_part, span_part], axis=0).transpose(1, 0, 2)
    rotated = rotate(queries.reshape(rows, width // head, head).astype(F32), positions)
    rotated = rotated.astype(BF16).reshape(rows, kv_local, width // kv_local).transpose(1, 0, 2)
    if nz > 1:
        local = lax.all_to_all(local, "z", 0, 0, tiled=True)
        rotated = lax.all_to_all(rotated, "z", 0, 0, tiled=True)
    entries = lax.all_gather(local, "j", axis=0, tiled=False)
    if nz % nt == 0 and nj & (nj - 1) == 0:
        return project(rotated, entries, lengths, out_weight, j, nz, nj, nt)
    attention = attend(rotated, entries, lengths, j, 0, 1)
    wide = attention.reshape(nz * rows, -1)
    wide = lax.all_gather(wide, ("z", "j"), axis=0, tiled=True)
    projected = jnp.dot(wide, out_weight, preferred_element_type=F32).astype(BF16)
    return lax.psum_scatter(projected, "tp", scatter_dimension=0, tiled=True)


def solution(mesh):
    nc, nt = mesh.shape["ctx"], mesh.shape["tp"]

    def run(queries, span_kv, cache_kv, out_weight, offset, lengths):
        kv_local = span_kv.shape[1] // nt
        nz = kv_local
        nj = nc // nz
        inner = Mesh(mesh.devices.reshape(nz, nj, nt), ("z", "j", "tp"))
        ctx = ("z", "j")
        call = jax.shard_map(
            functools.partial(body, nz=nz, nj=nj, nt=nt),
            mesh=inner,
            in_specs=(
                P(ctx, "tp"),
                P(ctx, "tp", None, None),
                P(ctx, "tp", None, None),
                P("tp", ctx),
                P(),
                P(),
            ),
            out_specs=P("tp", ctx),
            check_vma=False,
        )
        return call(queries, span_kv, cache_kv, out_weight, offset, lengths)

    return run
```

time: 1500 us -> 624 us (0.42)
  waiting for transfers between devices: 955 us -> 235 us
  matrix products: 341 us -> 38.8 us
  Pallas kernels: 0 us -> 244 us
  other arithmetic: 154 us -> 5.85 us
  blocking collectives: 0 us -> 43.3 us
  starting transfers between devices: 0.09 us -> 30.7 us
  local copies, waits for them, and re-layouts: 34.3 us -> 11.5 us
    all_gather x2 -> x3, waiting for transfers between devices: 941 us -> 129 us  [the longest x2 72 us: project(): wide.append(lax.all_gather(part, 'z', axis=2, tiled=True))]
    dot_general x13 -> x8, matrix products: 341 us -> 38.8 us  [project(): jnp.einsum('ctk,kn->ctn', wide[g], weights[r], preferred_element_type=F32)]
    pallas_call x0 -> x2, Pallas kernels: none -> 244 us  [attend(): pl.pallas_call(kernel, grid_spec=grid_spec, out_shape=jax.ShapeDtypeStruc...]
    reduce_sum x12 -> x0, other arithmetic: 131 us -> none  [the longest x6 130 us: online_update(): running_sum = running_sum * factor + jnp.sum(weights, axis=-1)]
    ppermute x0 -> x17, waiting for transfers between devices: none -> 107 us  [the longest x3 86 us: project(): weights.append(lax.ppermute(out_weight, 'j', swaps[r]))]
    all_to_all x0 -> x1, blocking collectives: none -> 43.3 us  [body(): local = lax.all_to_all(local, 'z', 0, 0, tiled=True)]
    ppermute x0 -> x17, starting transfers between devices: none -> 26.8 us  [the longest x3 17.2 us: project(): weights.append(lax.ppermute(out_weight, 'j', swaps[r]))]
    slice x3 -> x1, local copies, waits for them, and re-layouts: 25.2 us -> 0.73 us  [body(): span_keys = rotate(span_kv[:, :, 0, :].astype(F32), positions).astype(BF16)]
  transfers between devices with their start and end apart: 3 -> 21, of which waited for: 3 -> 7; matrix products, arithmetic and copies ran while one was open for 1% -> 8% of each run, Pallas kernels for 0% -> 18%
where the time goes in v1:
time: 624 us
  Pallas kernels  244 us (39%)
  waiting for transfers between devices  235 us (38%)
  blocking collectives  43.3 us (7%)
  matrix products  38.8 us (6%)
  starting transfers between devices  30.7 us (5%)
  between operations  14.3 us (2%)
  local copies, waits for them, and re-layouts  11.5 us (2%)
    pallas_call x2, Pallas kernels, attend(): pl.pallas_call(kernel, grid_spec=grid_spec, out_shape=jax.ShapeDtypeStruc...  244 us
    ppermute x3, waiting for transfers between devices, project(): weights.append(lax.ppermute(out_weight, 'j', swaps[r]))  86 us
    all_gather x2, waiting for transfers between devices, project(): wide.append(lax.all_gather(part, 'z', axis=2, tiled=True))  72 us
    all_gather x1, waiting for transfers between devices, body(): entries = lax.all_gather(local, 'j', axis=0, tiled=False)  56.6 us
    all_to_all x1, blocking collectives, body(): local = lax.all_to_all(local, 'z', 0, 0, tiled=True)  43.3 us
    dot_general x8, matrix products, project(): jnp.einsum('ctk,kn->ctn', wide[g], weights[r], preferred_element_type=F32)  38.8 us
    ppermute x6, waiting for transfers between devices, project(): total = lax.ppermute(total, 'j', swaps[r])  19.9 us
    ppermute x3, starting transfers between devices, project(): weights.append(lax.ppermute(out_weight, 'j', swaps[r]))  17.2 us
  transfers between devices with their start and end apart: 21, of which 7 were waited for; matrix products, arithmetic and copies ran while one was open for 8% of the time, Pallas kernels for 18%

profile of v1, /device:TPU:0, one launch (start us, length us, event | category | flops | bytes accessed | tf_op | source)
XLA Modules:
  0.0 623.6 jit_solution(16039525878046607900)
XLA Ops:
  7.3 0.3 multiply_cosine_fusion
  7.6 0.1 copy.21
  7.7 0.1 copy.22
  7.8 1.7 reshape.88
  9.5 0.1 copy.24
  9.7 0.7 fusion.37
  10.5 0.3 subtract_convert_fusion.1
  10.8 0.3 maximum_bitcast_fusion
  11.1 43.3 %all_to_all.10 = bf16[4,768,256]{2,1,0:T(8,128)(2,1)} all-to-all(bf16[4,768,256]{2,1,0:T(8,128)(2,1)S(1)} %maximum_bitcast_fusion), channel_id=1, replica_groups=mesh['z'=4,'j'=4,'tp'=2] {'z'}, dimensions={0} | all-to-all | bytes 3145728 | tf_op jit(solution)/shard_map/all_to_all | solution.py:245
  54.5 3.0 copy.17
  57.4 2.9 subtract_convert_fusion
  60.4 0.1 pad_maximum_fusion
  60.5 2.4 copy.18
  62.9 3.6 all-to-all-start
  66.5 0.7 pad_add_fusion.1.meta_ref
  67.2 56.6 %all-gather.9.cloned.1.call-done = bf16[16,768,256]{2,1,0:T(8,128)(2,1)} async-done(((bf16[4,768,256]{2,1,0:T(8,128)(2,1)}), bf16[16,768,256]{2,1,0:T(8,128)(2,1)}) %all-gather.9.cloned.1.call-update) | async-done | bytes 6291472 | tf_op jit(solution)/shard_map/all_gather | solution.py:247
  123.8 1.3 copy-done
  125.1 129.1 %attend.3 = bf16[2,256,1024]{2,1,0:T(8,128)(2,1)} custom-call(s32[2]{0:T(128)} %pad_add_fusion.1.meta_ref, s32[32]{0:T(128)} %len_ref.3, bf16[4,256,1024]{2,1,0:T(8,128)(2,1)} %copy-done, bf16[4,4,768,256]{3,2,1,0:T(8,128)(2,1)} %bitcast.122), custom_call_target="tpu_custom_call" | custom-call | tf_op jit(solution)/shard_map/attend/pallas_call | solution.py:189
  254.3 0.2 all-gather.5.cloned.1.call-start
  254.5 0.7 pad_add_fusion.meta_ref
  255.1 114.9 %attend.2 = bf16[2,256,1024]{2,1,0:T(8,128)(2,1)} custom-call(s32[2]{0:T(128)} %pad_add_fusion.meta_ref, s32[32]{0:T(128)} %len_ref.3, bf16[4,256,1024]{2,1,0:T(8,128)(2,1)} %copy-done, bf16[4,4,768,256]{3,2,1,0:T(8,128)(2,1)} %bitcast.123), custom_call_target="tpu_custom_call" | custom-call | tf_op jit(solution)/shard_map/attend/pallas_call | solution.py:189
  370.1 15.8 %collective-permute-start.7 = (bf16[4096,512]{1,0:T(8,128)(2,1)}, bf16[4096,512]{1,0:T(8,128)(2,1)}, u32[]{:S(2)}, u32[]{:S(2)}) collective-permute-start(bf16[4096,512]{1,0:T(8,128)(2,1)} %param.9), channel_id=1, source_target_pairs={{0,6},{2,4},{4,2},{6,0},{1,7},{3,5},{5,3},{7,1},{8,14},{10,12},{12... | collective-permute-start | bytes 12582920 | tf_op jit(solution)/shard_map/ppermute | solution.py:206
  385.9 0.1 collective-permute-start.4
  385.9 1.4 collective-permute-start.1
  387.3 5.8 fusion.12
  393.3 72.0 %all-gather.5.cloned.1.call-done = bf16[2,256,4096]{2,1,0:T(8,128)(2,1)} async-done(((bf16[2,256,1024]{2,1,0:T(8,128)(2,1)}), bf16[2,256,4096]{2,1,0:T(8,128)(2,1)}) %all-gather.5.cloned.1.call-update) | async-done | bytes 4194320 | tf_op jit(solution)/shard_map/all_gather | solution.py:210
  465.2 5.9 fusion.14
  471.3 6.4 %collective-permute-done.7 = bf16[4096,512]{1,0:T(8,128)(2,1)} collective-permute-done((bf16[4096,512]{1,0:T(8,128)(2,1)}, bf16[4096,512]{1,0:T(8,128)(2,1)}, u32[]{:S(2)}, u32[]{:S(2)}) %collective-permute-start.7) | collective-permute-done | bytes 4194336 | tf_op jit(solution)/shard_map/ppermute | solution.py:206
  477.6 4.5 fusion
  482.3 4.5 fusion.2
  486.9 79.6 %collective-permute-done.4 = bf16[4096,512]{1,0:T(8,128)(2,1)} collective-permute-done((bf16[4096,512]{1,0:T(8,128)(2,1)}, bf16[4096,512]{1,0:T(8,128)(2,1)}, u32[]{:S(2)}, u32[]{:S(2)}) %collective-permute-start.4) | collective-permute-done | bytes 4194336 | tf_op jit(solution)/shard_map/ppermute | solution.py:206
  566.5 4.5 fusion.6
  571.0 4.5 fusion.4
  575.6 0.6 collective-permute-start.13
  576.2 4.5 fusion.8
  580.7 4.5 fusion.10
  585.5 0.6 collective-permute-start.11
  586.3 0.6 collective-permute-done.5
  586.9 2.6 collective-permute-start.16
  589.6 0.7 collective-permute-start.9
  590.5 1.2 collective-permute-start.3
  591.7 1.8 collective-permute-start.6
  593.5 0.2 broadcast_in_dim.35
  593.8 14.0 %collective-permute-done.3 = bf16[256,512]{1,0:T(8,128)(2,1)S(1)} collective-permute-done((bf16[256,512]{1,0:T(8,128)(2,1)S(1)}, bf16[256,512]{1,0:T(8,128)(2,1)S(1)}, u32[]{:S(2)}, u32[]{:S(2)}) %collective-permute-start.3) | collective-permute-done | bytes 262176 | tf_op jit(solution)/shard_map/ppermute | solution.py:225
  607.8 0.2 collective-permute-start.14
  608.0 1.5 collective-permute-start.12
  609.7 5.9 collective-permute-done.12
  615.7 1.3 copy-done.2
  (61 shorter events, 1.7 us)
Async XLA Ops:
  6.5 3.1 copy-start.3
  6.5 117.3 %all-gather.9.cloned.1.call-start = ((), (), s32[]{:S(2)}) async-start(), calls=%async_computation.4 | async-start | bytes 7864320 | tf_op jit(solution)/shard_map/all_gather | solution.py:247
  10.8 43.7 %copy-start.1 = (bf16[256,4096]{1,0:T(8,128)(2,1)S(1)}, bf16[256,4096]{1,0:T(8,128)(2,1)}, u32[]{:S(2)}) copy-start(bf16[256,4096]{1,0:T(8,128)(2,1)} %param.6) | copy-start | bytes 6291460
  62.9 60.9 %all-to-all-start = ((bf16[4,256,1024]{2,1,0:T(8,128)(2,1)}), bf16[4,256,1024]{2,1,0:T(8,128)(2,1)S(1)}, u32[]{:S(2)}, u32[]{:S(2)}) async-start(bf16[4,256,1024]{2,1,0:T(8,128)(2,1)} %bitcast.125), calls=%async_computation | async-start | bytes 4194304 | tf_op jit(solution)/shard_map/all_to_all | solution.py:246
  66.5 320.8 %all-gather.7.cloned.1.call-start = ((), (), s32[]{:S(2)}) async-start(), calls=%async_computation.3 | async-start | bytes 5242880 | tf_op jit(solution)/shard_map/all_gather | solution.py:210
  123.8 1.3 copy-start
  254.3 211.0 %all-gather.5.cloned.1.call-start = ((), (), s32[]{:S(2)}) async-start(), calls=%async_computation.2 | async-start | bytes 5242880 | tf_op jit(solution)/shard_map/all_gather | solution.py:210
  370.1 107.6 %collective-permute-start.7 = (bf16[4096,512]{1,0:T(8,128)(2,1)}, bf16[4096,512]{1,0:T(8,128)(2,1)}, u32[]{:S(2)}, u32[]{:S(2)}) collective-permute-start(bf16[4096,512]{1,0:T(8,128)(2,1)} %param.9), channel_id=1, source_target_pairs={{0,6},{2,4},{4,2},{6,0},{1,7},{3,5},{5,3},{7,1},{8,14},{10,12},{12... | collective-permute-start | bytes 12582920 | tf_op jit(solution)/shard_map/ppermute | solution.py:206
  385.9 180.6 %collective-permute-start.4 = (bf16[4096,512]{1,0:T(8,128)(2,1)}, bf16[4096,512]{1,0:T(8,128)(2,1)}, u32[]{:S(2)}, u32[]{:S(2)}) collective-permute-start(bf16[4096,512]{1,0:T(8,128)(2,1)} %param.9), channel_id=1, source_target_pairs={{0,4},{2,6},{4,0},{6,2},{1,5},{3,7},{5,1},{7,3},{8,12},{10,14},{12... | collective-permute-start | bytes 12582920 | tf_op jit(solution)/shard_map/ppermute | solution.py:206
  385.9 189.7 %collective-permute-start.1 = (bf16[4096,512]{1,0:T(8,128)(2,1)}, bf16[4096,512]{1,0:T(8,128)(2,1)}, u32[]{:S(2)}, u32[]{:S(2)}) collective-permute-start(bf16[4096,512]{1,0:T(8,128)(2,1)} %param.9), channel_id=1, source_target_pairs={{0,2},{2,0},{4,6},{6,4},{1,3},{3,1},{5,7},{7,5},{8,10},{10,8},{12,... | collective-permute-start | bytes 12582920 | tf_op jit(solution)/shard_map/ppermute | solution.py:206
  393.2 216.5 %collective-permute-start.10 = (bf16[256,512]{1,0:T(8,128)(2,1)S(1)}, bf16[256,512]{1,0:T(8,128)(2,1)S(1)}, u32[]{:S(2)}, u32[]{:S(2)}) collective-permute-start(bf16[256,512]{1,0:T(8,128)(2,1)S(1)} %fusion.28), channel_id=1, source_target_pairs={{0,1},{1,0},{2,3},{3,2},{4,5},{5,4},{6,7},{7,6},{8,9},{9,8},{10,11... | collective-permute-start | bytes 786440 | tf_op jit(solution)/shard_map/ppermute | solution.py:221
  465.2 12.4 %copy-start.4 = (bf16[2,256,4096]{2,1,0:T(8,128)(2,1)S(1)}, bf16[2,256,4096]{2,1,0:T(8,128)(2,1)}, u32[]{:S(2)}) copy-start(bf16[2,256,4096]{2,1,0:T(8,128)(2,1)} %all-gather.7.cloned.1.call-done) | copy-start | bytes 12582916
  471.2 11.1 %copy-start.5 = (bf16[2,256,4096]{2,1,0:T(8,128)(2,1)S(1)}, bf16[2,256,4096]{2,1,0:T(8,128)(2,1)}, u32[]{:S(2)}) copy-start(bf16[2,256,4096]{2,1,0:T(8,128)(2,1)} %all-gather.5.cloned.1.call-done) | copy-start | bytes 12582916
  471.2 120.5 %collective-permute-start = (bf16[256,512]{1,0:T(8,128)(2,1)S(1)}, bf16[256,512]{1,0:T(8,128)(2,1)S(1)}, u32[]{:S(2)}, u32[]{:S(2)}) collective-permute-start(bf16[256,512]{1,0:T(8,128)(2,1)S(1)} %fusion.24), channel_id=1, source_target_pairs={{0,1},{1,0},{2,3},{3,2},{4,5},{5,4},{6,7},{7,6},{8,9},{9,8},{10,11... | collective-permute-start | bytes 786440 | tf_op jit(solution)/shard_map/ppermute | solution.py:221
  482.2 103.1 %collective-permute-start.15 = (bf16[256,512]{1,0:T(8,128)(2,1)S(1)}, bf16[256,512]{1,0:T(8,128)(2,1)S(1)}, u32[]{:S(2)}, u32[]{:S(2)}) collective-permute-start(bf16[256,512]{1,0:T(8,128)(2,1)S(1)} %fusion.31), channel_id=1, source_target_pairs={{0,1},{1,0},{2,3},{3,2},{4,5},{5,4},{6,7},{7,6},{8,9},{9,8},{10,11... | collective-permute-start | bytes 786440 | tf_op jit(solution)/shard_map/ppermute | solution.py:221
  566.5 19.0 %collective-permute-start.8 = (bf16[256,512]{1,0:T(8,128)(2,1)S(1)}, bf16[256,512]{1,0:T(8,128)(2,1)S(1)}, u32[]{:S(2)}, u32[]{:S(2)}) collective-permute-start(bf16[256,512]{1,0:T(8,128)(2,1)S(1)} %fusion.27), channel_id=1, source_target_pairs={{0,1},{1,0},{2,3},{3,2},{4,5},{5,4},{6,7},{7,6},{8,9},{9,8},{10,11... | collective-permute-start | bytes 786440 | tf_op jit(solution)/shard_map/ppermute | solution.py:221
  575.6 10.5 %collective-permute-start.13 = (bf16[256,512]{1,0:T(8,128)(2,1)S(1)}, bf16[256,512]{1,0:T(8,128)(2,1)S(1)}, u32[]{:S(2)}, u32[]{:S(2)}) collective-permute-start(bf16[256,512]{1,0:T(8,128)(2,1)S(1)} %fusion.30), channel_id=1, source_target_pairs={{0,1},{1,0},{2,3},{3,2},{4,5},{5,4},{6,7},{7,6},{8,9},{9,8},{10,11... | collective-permute-start | bytes 786440 | tf_op jit(solution)/shard_map/ppermute | solution.py:221
  585.3 1.6 collective-permute-start.5
  585.5 5.0 collective-permute-start.11
  586.1 3.5 collective-permute-start.2
  586.9 28.8 %collective-permute-start.16 = (bf16[256,512]{1,0:T(8,128)(2,1)S(1)}, bf16[256,512]{1,0:T(8,128)(2,1)S(1)}, u32[]{:S(2)}, u32[]{:S(2)}) collective-permute-start(bf16[256,512]{1,0:T(8,128)(2,1)S(1)} %fusion.16), channel_id=1, source_target_pairs={{0,6},{2,4},{4,2},{6,0},{1,7},{3,5},{5,3},{7,1},{8,14},{10,12},{12... | collective-permute-start | bytes 786440 | tf_op jit(solution)/shard_map/ppermute | solution.py:225
  589.6 20.0 %collective-permute-start.9 = (bf16[256,512]{1,0:T(8,128)(2,1)S(1)}, bf16[256,512]{1,0:T(8,128)(2,1)S(1)}, u32[]{:S(2)}, u32[]{:S(2)}) collective-permute-start(bf16[256,512]{1,0:T(8,128)(2,1)S(1)} %fusion.20), channel_id=1, source_target_pairs={{0,6},{2,4},{4,2},{6,0},{1,7},{3,5},{5,3},{7,1},{8,14},{10,12},{12... | collective-permute-start | bytes 786440 | tf_op jit(solution)/shard_map/ppermute | solution.py:225
  590.5 17.4 %collective-permute-start.3 = (bf16[256,512]{1,0:T(8,128)(2,1)S(1)}, bf16[256,512]{1,0:T(8,128)(2,1)S(1)}, u32[]{:S(2)}, u32[]{:S(2)}) collective-permute-start(bf16[256,512]{1,0:T(8,128)(2,1)S(1)} %fusion.22), channel_id=1, source_target_pairs={{0,2},{2,0},{4,6},{6,4},{1,3},{3,1},{5,7},{7,5},{8,10},{10,8},{12,... | collective-permute-start | bytes 786440 | tf_op jit(solution)/shard_map/ppermute | solution.py:225
  591.7 16.3 %collective-permute-start.6 = (bf16[256,512]{1,0:T(8,128)(2,1)S(1)}, bf16[256,512]{1,0:T(8,128)(2,1)S(1)}, u32[]{:S(2)}, u32[]{:S(2)}) collective-permute-start(bf16[256,512]{1,0:T(8,128)(2,1)S(1)} %fusion.21), channel_id=1, source_target_pairs={{0,4},{2,6},{4,0},{6,2},{1,5},{3,7},{5,1},{7,3},{8,12},{10,14},{12... | collective-permute-start | bytes 786440 | tf_op jit(solution)/shard_map/ppermute | solution.py:225
  607.8 7.8 %collective-permute-start.14 = (bf16[256,512]{1,0:T(8,128)(2,1)S(1)}, bf16[256,512]{1,0:T(8,128)(2,1)S(1)}, u32[]{:S(2)}, u32[]{:S(2)}) collective-permute-start(bf16[256,512]{1,0:T(8,128)(2,1)S(1)} %fusion.17), channel_id=1, source_target_pairs={{0,4},{2,6},{4,0},{6,2},{1,5},{3,7},{5,1},{7,3},{8,12},{10,14},{12... | collective-permute-start | bytes 786440 | tf_op jit(solution)/shard_map/ppermute | solution.py:225
  608.0 7.6 %collective-permute-start.12 = (bf16[256,512]{1,0:T(8,128)(2,1)S(1)}, bf16[256,512]{1,0:T(8,128)(2,1)S(1)}, u32[]{:S(2)}, u32[]{:S(2)}) collective-permute-start(bf16[256,512]{1,0:T(8,128)(2,1)S(1)} %fusion.18), channel_id=1, source_target_pairs={{0,2},{2,0},{4,6},{6,4},{1,3},{3,1},{5,7},{7,5},{8,10},{10,8},{12,... | collective-permute-start | bytes 786440 | tf_op jit(solution)/shard_map/ppermute | solution.py:225
  615.7 1.3 copy-start.2
Sparse Core Ops, SparseCore 0:
  54.6 69.1 all-gather.8
  254.4 87.8 all-gather.6
  370.2 94.9 all-gather.4

commit v2 on v1

--- a/solution.py
+++ b/solution.py
@@ -39,19 +39,18 @@
 
 
 def square_bound(rows):
-    squares = (rows * rows).astype(BF16)
+    squares = rows * rows
     ones = jnp.ones((rows.shape[1], rows.shape[1]), BF16)
     sums = jnp.dot(squares, ones, preferred_element_type=F32)
     return jnp.max(sums, axis=0, keepdims=True)
 
 
-def attend(queries, entries, lengths, j, start, stride):
-    chunks, rows, width = queries.shape
-    count = chunks // stride
+def attend(queries, entries, lengths, j, start, stride, count):
+    _, rows, width = queries.shape
     nj, nz, local, pair = entries.shape
+    cached = local - rows
     head = pair // 2
     group = width // head
-    cached = local - rows
     shards = nj * nz
     slots = lengths.shape[0]
     slot = cached * shards // slots
@@ -60,6 +59,8 @@
     block = key_rows
     span_blocks = span // block
     stack = group * rows
+    slice_rows = min(stack, 512)
+    slow_rows = min(stack, 256)
     scale = math.log2(math.e) / math.sqrt(head)
     capacity = span + shards * cached + block
 
@@ -72,11 +73,11 @@
 
             def put_span(shard, carry):
                 place = pl.ds(pl.multiple_of(shard * rows, rows), rows)
-                piece = kv_ref[shard % nj, shard // nj, pl.ds(cached, rows), :]
+                piece = kv_ref[shard % nj, shard // nj, cached:, :]
                 keys[place, :] = piece[:, :head]
                 values[place, :head] = piece[:, head:]
                 values[place, head:] = jnp.ones((rows, head), BF16)
-                norms[...] = jnp.maximum(norms[...], square_bound(piece[:, :head].astype(F32)))
+                norms[...] = jnp.maximum(norms[...], square_bound(piece[:, :head]))
                 return carry
 
             lax.fori_loop(0, shards, put_span, 0)
@@ -85,15 +86,13 @@
             def put_slot(number, at):
                 shard = number // per_shard
                 inside = pl.multiple_of((number % per_shard) * slot, slot)
-                piece = kv_ref[shard % nj, shard // nj, pl.ds(inside, slot), :].astype(F32)
+                piece = kv_ref[shard % nj, shard // nj, pl.ds(inside, slot), :]
                 size = len_ref[number]
-                valid = index < size
-                fixed = jnp.where(valid, piece[:, :head], piece[0:1, :head])
                 place = pl.ds(pl.multiple_of(at, 16), slot)
-                keys[place, :] = fixed.astype(BF16)
-                values[place, :head] = jnp.where(valid, piece[:, head:], 0.0).astype(BF16)
-                values[place, head:] = jnp.where(valid, 1.0, 0.0).astype(BF16)
-                norms[...] = jnp.maximum(norms[...], square_bound(fixed))
+                keys[place, :] = piece[:, :head]
+                values[place, :head] = piece[:, head:]
+                values[place, head:] = jnp.where(index < size, 1.0, 0.0).astype(BF16)
+                norms[...] = jnp.maximum(norms[...], square_bound(piece[:, :head]))
                 return at + (size + 15) // 16 * 16
 
             end = lax.fori_loop(0, slots, put_slot, span)
@@ -109,59 +108,82 @@
         first_token = (meta_ref[0] + (meta_ref[1] + step * stride) * nj) * rows
         full = first_token // block
         total = full + counts[0]
-        query_bound = jnp.max(square_bound(stacked[...].astype(F32)))
-        safe = query_bound * bounds[0] * (1.05 * scale * scale) <= bound_limit * bound_limit
-
-        def scores_of(at):
+        query_bound = jnp.max(square_bound(stacked[...]))
+        safe = query_bound * bounds[0] * (1.03 * scale * scale) <= bound_limit * bound_limit
+
+        def scores_of(at, part):
             raw = lax.dot_general(
-                stacked[...],
+                stacked[part, :],
                 keys[pl.ds(at, block), :],
                 (((1,), (1,)), ((), ())),
                 preferred_element_type=F32,
             )
             return raw * scale
 
-        token = first_token + lax.broadcasted_iota(jnp.int32, (stack, block), 0) % rows
-        column = lax.broadcasted_iota(jnp.int32, (stack, block), 1)
+        def masked_of(at, part, first):
+            token = first_token + (first + lax.broadcasted_iota(jnp.int32, (slice_rows, block), 0)) % rows
+            column = lax.broadcasted_iota(jnp.int32, (slice_rows, block), 1)
+            return jnp.where(at + column <= token, scores_of(at, part), lowest_score)
 
         def place_of(i):
             return pl.multiple_of(jnp.where(i < full, i, span_blocks + i - full) * block, block)
 
-        def add_plain(at, scores):
+        def part_of(n, size):
+            first = pl.multiple_of(n * size, size)
+            return pl.ds(first, size), first
+
+        last = pl.multiple_of(full * block, block)
+
+        def add_plain(at, part, scores):
             weights = jnp.exp2(scores).astype(BF16)
-            acc[...] += jnp.dot(weights, values[pl.ds(at, block), :], preferred_element_type=F32)
+            acc[part, :] += jnp.dot(weights, values[pl.ds(at, block), :], preferred_element_type=F32)
 
         @pl.when(safe)
         def _():
             def body(i, carry):
                 at = place_of(i)
-                add_plain(at, scores_of(at))
+                whole = slice(0, stack)
+                add_plain(at, whole, scores_of(at, whole))
                 return carry
 
             lax.fori_loop(0, total, body, 0)
-            at = pl.multiple_of(full * block, block)
-            add_plain(at, jnp.where(at + column <= token, scores_of(at), lowest_score))
+
+            def edge(n, carry):
+                part, first = part_of(n, slice_rows)
+                add_plain(last, part, masked_of(last, part, first))
+                return carry
+
+            lax.fori_loop(0, stack // slice_rows, edge, 0)
 
         @pl.when(jnp.logical_not(safe))
         def _():
             top[...] = jnp.full_like(top, lowest_score)
 
-            def body(i, carry):
-                last = i == total
-                at = jnp.where(last, pl.multiple_of(full * block, block), place_of(i))
-                at = pl.multiple_of(at, block)
-                entry = jnp.where(last, at, -block) + column
-                scores = jnp.where(entry <= token, scores_of(at), lowest_score)
-                before = top[...]
+            def add_online(at, part, scores):
+                before = top[part, :]
                 now = jnp.maximum(before, jnp.max(scores, axis=1, keepdims=True))
                 factor = jnp.exp2(before - now)
                 weights = jnp.exp2(scores - now[:, :1]).astype(BF16)
                 fresh = jnp.dot(weights, values[pl.ds(at, block), :], preferred_element_type=F32)
-                acc[...] = acc[...] * jnp.concatenate([factor, factor], axis=1) + fresh
-                top[...] = now
+                acc[part, :] = acc[part, :] * jnp.concatenate([factor, factor], axis=1) + fresh
+                top[part, :] = now
+
+            def rows_body(n, carry):
+                part, first = part_of(n, slow_rows)
+
+                def body(i, inner):
+                    edge_block = i == total
+                    at = pl.multiple_of(jnp.where(edge_block, last, place_of(i)), block)
+                    token = first_token + (first + lax.broadcasted_iota(jnp.int32, (slow_rows, block), 0)) % rows
+                    column = lax.broadcasted_iota(jnp.int32, (slow_rows, block), 1)
+                    entry = jnp.where(edge_block, last, -block) + column
+                    add_online(at, part, jnp.where(entry <= token, scores_of(at, part), lowest_score))
+                    return inner
+
+                lax.fori_loop(0, total + 1, body, 0)
                 return carry
 
-            lax.fori_loop(0, total + 1, body, 0)
+            lax.fori_loop(0, stack // slow_rows, rows_body, 0)
 
         for g in range(group):
             part = slice(g * rows, (g + 1) * rows)
@@ -195,36 +217,53 @@
     )(jnp.stack([j, jnp.int32(start)]).astype(jnp.int32), lengths, queries, entries)
 
 
-def project(rotated, entries, lengths, out_weight, j, nz, nj, nt):
+def project(rotated, entries, lengths, out_weight, j, nz, nt):
+    nj = entries.shape[0]
     groups = nz // nt
     rows, columns = rotated.shape[1], out_weight.shape[1]
+    half = out_weight.shape[0] // 2
     tp = lax.axis_index("tp")
     entries, out_weight = lax.optimization_barrier((entries, out_weight))
-    swaps = [[(i, i ^ r) for i in range(nj)] for r in range(nj)]
-    weights = [out_weight]
-    for r in range(1, nj):
-        weights.append(lax.ppermute(out_weight, "j", swaps[r]))
-    wide = []
+    near = move(1, out_weight)
+    far = move(2, out_weight)
+    pieces = []
     for g in range(groups):
-        part = attend(rotated, entries, lengths, j, g, groups)
-        wide.append(lax.all_gather(part, "z", axis=2, tiled=True))
+        calls = [(owner, 1) for owner in reversed(range(nt))] if g < groups - 1 else [(0, nt)]
+        for owner, count in calls:
+            part = attend(rotated, entries, lengths, j, owner * groups + g, groups, count)
+            pieces.append(lax.all_gather(part, "z", axis=2, tiled=True))
+    across = (move(1, far[:half]), move(2, near[half:]))
+    weights = [(out_weight,), (near,), (far,), across]
+
+    def times(left, r):
+        if len(weights[r]) == 1:
+            return jnp.einsum("ctk,kn->ctn", left, weights[r][0], preferred_element_type=F32)
+        first = jnp.einsum("ctk,kn->ctn", left[..., :half], weights[r][0], preferred_element_type=F32)
+        return first + jnp.einsum("ctk,kn->ctn", left[..., half:], weights[r][1], preferred_element_type=F32)
+
     out = jnp.zeros((groups, nj, rows, columns), BF16)
-    ready = []
     for g in range(groups):
-        wide[g], ready = lax.optimization_barrier((wide[g], ready))
-        for r in [0] + list(range(1, nj)):
-            partial = jnp.einsum("ctk,kn->ctn", wide[g], weights[r], preferred_element_type=F32)
-            total = lax.dynamic_index_in_dim(partial, tp, 0, keepdims=False)
+        lefts = pieces[g * nt : (g + 1) * nt][::-1] if g < groups - 1 else pieces[g * nt :]
+        for r in [0, 1, 2, 3] if g < groups - 1 else [3, 1, 2, 0]:
+            parts = []
+            for left in lefts:
+                parts.append(times(left, r))
+            chunks = jnp.concatenate(parts) if len(parts) > 1 else parts[0]
+            total = lax.dynamic_index_in_dim(chunks, tp, 0, keepdims=False)
             for step in range(1, nt):
                 turn = [(i, (i + step) % nt) for i in range(nt)]
-                away = lax.dynamic_index_in_dim(partial, (tp + step) % nt, 0, keepdims=False)
-                total = total + lax.ppermute(away.astype(BF16), "tp", turn).astype(F32)
+                away = lax.dynamic_index_in_dim(chunks, (tp + step) % nt, 0, keepdims=False)
+                away = lax.ppermute(away.astype(BF16), "tp", turn)
+                total = total + away.astype(F32)
             total = total.astype(BF16)
-            ready.append(total[:1, :1])
             if r:
-                total = lax.ppermute(total, "j", swaps[r])
+                total = move(r, total)
             out = lax.dynamic_update_slice(out, total[None, None], (g, j ^ r, 0, 0))
     return out.reshape(groups * nj * rows, columns)
+
+
+def move(r, array):
+    return lax.ppermute(array, "j", [(i, i ^ r) for i in range(4)])
 
 
 def body(queries, span_kv, cache_kv, out_weight, offset, lengths, *, nz, nj, nt):
@@ -236,18 +275,28 @@
     positions = offset[0] + (z * nj + j) * rows + jnp.arange(rows, dtype=jnp.int32)
 
     span_keys = rotate(span_kv[:, :, 0, :].astype(F32), positions).astype(BF16)
-    span_part = jnp.concatenate([span_keys, span_kv[:, :, 1, :]], axis=-1)
-    cache_part = cache_kv.reshape(cached, kv_local, 2 * head)
-    local = jnp.concatenate([cache_part, span_part], axis=0).transpose(1, 0, 2)
+    span = jnp.concatenate([span_keys, span_kv[:, :, 1, :]], axis=-1)
+    slots = lengths.shape[0] // (nz * nj)
+    sizes = lax.dynamic_slice_in_dim(lengths, (z * nj + j) * slots, slots)
+    cache = cache_kv.reshape(slots, cached // slots, kv_local, 2 * head)
+    inside = jnp.arange(cached // slots, dtype=jnp.int32)
+    valid = (inside[None, :] < sizes[:, None])[:, :, None, None]
+    is_key = jnp.arange(2 * head, dtype=jnp.int32) < head
+    filler = jnp.where(is_key, cache[:, :1], jnp.zeros((), BF16))
+    cache = jnp.where(valid, cache, filler).reshape(cached, kv_local, 2 * head)
+    local = jnp.concatenate([cache, span], axis=0).transpose(1, 0, 2)
     rotated = rotate(queries.reshape(rows, width // head, head).astype(F32), positions)
     rotated = rotated.astype(BF16).reshape(rows, kv_local, width // kv_local).transpose(1, 0, 2)
+    split = nz % nt == 0 and nj == 4
     if nz > 1:
         local = lax.all_to_all(local, "z", 0, 0, tiled=True)
+        rotated, local = lax.optimization_barrier((rotated, local))
         rotated = lax.all_to_all(rotated, "z", 0, 0, tiled=True)
     entries = lax.all_gather(local, "j", axis=0, tiled=False)
-    if nz % nt == 0 and nj & (nj - 1) == 0:
-        return project(rotated, entries, lengths, out_weight, j, nz, nj, nt)
-    attention = attend(rotated, entries, lengths, j, 0, 1)
+
+    if split:
+        return project(rotated, entries, lengths, out_weight, j, nz, nt)
+    attention = attend(rotated, entries, lengths, j, 0, 1, nz)
     wide = attention.reshape(nz * rows, -1)
     wide = lax.all_gather(wide, ("z", "j"), axis=0, tiled=True)
     projected = jnp.dot(wide, out_weight, preferred_element_type=F32).astype(BF16)

time: 624 us -> 682 us (1.093)
  Pallas kernels: 244 us -> 384 us
  waiting for transfers between devices: 235 us -> 156 us
  blocking collectives: 43.3 us -> 0 us
  starting transfers between devices: 30.7 us -> 46 us
  matrix products: 38.8 us -> 53 us
  local copies, waits for them, and re-layouts: 11.5 us -> 19 us
    pallas_call x2 -> x3, Pallas kernels: 244 us -> 384 us  [attend(): pl.pallas_call(kernel, grid_spec=grid_spec, out_shape=jax.ShapeDtypeStruc...]
    ppermute x17 -> x18, waiting for transfers between devices: 107 us -> 14.9 us  [the longest x10 14.9 us: move(): return lax.ppermute(array, 'j', [(i, i ^ r) for i in range(4)])]
    all_to_all x1 -> x0, blocking collectives: 43.3 us -> none  [body(): local = lax.all_to_all(local, 'z', 0, 0, tiled=True)]
    all_to_all x0 -> x1, waiting for transfers between devices: none -> 28.7 us  [body(): local = lax.all_to_all(local, 'z', 0, 0, tiled=True)]
    all_gather x2 -> x3, waiting for transfers between devices: 72 us -> 46.9 us  [project(): pieces.append(lax.all_gather(part, 'z', axis=2, tiled=True))]
    dot_general x8 -> x15, matrix products: 38.8 us -> 53 us  [the longest x9 37.9 us: times(): jnp.einsum('ctk,kn->ctn', left, weights[r][0], preferred_element_type=F32)]
    ppermute x17 -> x18, starting transfers between devices: 26.8 us -> 35.6 us  [the longest x10 33.4 us: move(): return lax.ppermute(array, 'j', [(i, i ^ r) for i in range(4)])]
    all_gather x1, waiting for transfers between devices: 56.6 us -> 65 us  [body(): entries = lax.all_gather(local, 'j', axis=0, tiled=False)]
  transfers between devices with their start and end apart: 21 -> 24, of which waited for: 7 -> 6; matrix products, arithmetic and copies ran while one was open for 8% -> 10% of each run, Pallas kernels for 18% -> 44%
where the time goes in v2:
time: 682 us; the launch traced here: 681 us
  Pallas kernels  384 us (56%)
  waiting for transfers between devices  156 us (23%)
  matrix products  53 us (8%)
  starting transfers between devices  46 us (7%)
  local copies, waits for them, and re-layouts  19 us (3%)
  between operations  14.3 us (2%)
  other arithmetic  9.25 us (1%)
    pallas_call x3, Pallas kernels, attend(): pl.pallas_call(kernel, grid_spec=grid_spec, out_shape=jax.ShapeDtypeStruc...  384 us
    all_gather x1, waiting for transfers between devices, body(): entries = lax.all_gather(local, 'j', axis=0, tiled=False)  65 us
    all_gather x3, waiting for transfers between devices, project(): pieces.append(lax.all_gather(part, 'z', axis=2, tiled=True))  46.9 us
    dot_general x9, matrix products, times(): jnp.einsum('ctk,kn->ctn', left, weights[r][0], preferred_element_type=F32)  37.9 us
    ppermute x10, starting transfers between devices, move(): return lax.ppermute(array, 'j', [(i, i ^ r) for i in range(4)])  33.4 us
    all_to_all x1, waiting for transfers between devices, body(): local = lax.all_to_all(local, 'z', 0, 0, tiled=True)  28.7 us
    ppermute x10, waiting for transfers between devices, move(): return lax.ppermute(array, 'j', [(i, i ^ r) for i in range(4)])  14.9 us
  transfers between devices with their start and end apart: 24, of which 6 were waited for; matrix products, arithmetic and copies ran while one was open for 10% of the time, Pallas kernels for 44%

profile of v2, /device:TPU:0, one launch (start us, length us, event | category | flops | bytes accessed | tf_op | source)
XLA Modules:
  0.0 680.9 jit_solution(1694730763290877755)
XLA Ops:
  6.6 2.6 reshape.140
  9.2 0.7 reshape.156
  11.3 0.7 fusion.92
  12.0 0.7 fusion.93
  13.3 1.5 maximum_bitcast_fusion
  14.8 6.5 all-to-all-start
  21.2 3.0 copy.19
  24.2 2.9 subtract_convert_fusion
  27.3 2.4 copy.20
  29.6 28.7 %all-to-all-done = bf16[4,768,256]{2,1,0:T(8,128)(2,1)} async-done(((bf16[4,768,256]{2,1,0:T(8,128)(2,1)}), bf16[4,768,256]{2,1,0:T(8,128)(2,1)}, u32[]{:S(2)}, u32[]{:S(2)}) %all-to-all-start) | async-done | bytes 1572896 | tf_op jit(solution)/shard_map/all_to_all | solution.py:292
  58.3 3.6 all-to-all-start.1
  62.6 65.0 %all-gather.12.cloned.1.call-done = bf16[16,768,256]{2,1,0:T(8,128)(2,1)} async-done(((bf16[4,768,256]{2,1,0:T(8,128)(2,1)}), bf16[16,768,256]{2,1,0:T(8,128)(2,1)}) %all-gather.12.cloned.1.call-update) | async-done | bytes 6291472 | tf_op jit(solution)/shard_map/all_gather | solution.py:295
  127.6 1.3 copy-done
  128.9 81.9 %attend.3 = bf16[1,256,1024]{2,1,0:T(8,128)(2,1)} custom-call(s32[2]{0:T(128)} %pad_add_fusion.meta_ref, s32[32]{0:T(128)} %len_ref.5, bf16[4,256,1024]{2,1,0:T(8,128)(2,1)} %copy-done, bf16[4,4,768,256]{3,2,1,0:T(8,128)(2,1)} %bitcast.190), custom_call_target="tpu_custom_call" | custom-call | tf_op jit(solution)/shard_map/attend/pallas_call | solution.py:211
  210.9 0.7 pad_add_fusion.1.meta_ref
  211.6 104.6 %attend.4 = bf16[1,256,1024]{2,1,0:T(8,128)(2,1)} custom-call(s32[2]{0:T(128)} %pad_add_fusion.1.meta_ref, s32[32]{0:T(128)} %len_ref.5, bf16[4,256,1024]{2,1,0:T(8,128)(2,1)} %copy-done, bf16[4,4,768,256]{3,2,1,0:T(8,128)(2,1)} %bitcast.191), custom_call_target="tpu_custom_call" | custom-call | tf_op jit(solution)/shard_map/attend/pallas_call | solution.py:211
  316.5 1.5 collective-permute-start.1
  318.0 11.9 %collective-permute-start.4 = (bf16[4096,512]{1,0:T(8,128)(2,1)}, bf16[4096,512]{1,0:T(8,128)(2,1)}, u32[]{:S(2)}, u32[]{:S(2)}) collective-permute-start(bf16[4096,512]{1,0:T(8,128)(2,1)} %param.9), channel_id=1, source_target_pairs={{0,4},{2,6},{4,0},{6,2},{1,5},{3,7},{5,1},{7,3},{8,12},{10,14},{12... | collective-permute-start | bytes 12582920 | tf_op jit(solution)/shard_map/ppermute | solution.py:266
  330.5 197.2 %attend.5 = bf16[2,256,1024]{2,1,0:T(8,128)(2,1)} custom-call(s32[2]{0:T(128)} %pad_add_fusion.2.meta_ref, s32[32]{0:T(128)} %len_ref.5, bf16[4,256,1024]{2,1,0:T(8,128)(2,1)} %copy-done, bf16[4,4,768,256]{3,2,1,0:T(8,128)(2,1)} %bitcast.192), custom_call_target="tpu_custom_call" | custom-call | tf_op jit(solution)/shard_map/attend/pallas_call | solution.py:211
  527.8 4.1 fusion.31
  531.9 4.2 fusion.40
  536.1 3.6 fusion.43
  539.8 3.5 fusion.34
  543.5 3.7 fusion.46
  547.2 3.8 fusion.37
  552.0 1.4 collective-permute-start.3
  553.6 11.3 %collective-permute-start.6 = (bf16[256,512]{1,0:T(8,128)(2,1)S(1)}, bf16[256,512]{1,0:T(8,128)(2,1)S(1)}, u32[]{:S(2)}, u32[]{:S(2)}) collective-permute-start(bf16[256,512]{1,0:T(8,128)(2,1)S(1)} %fusion.62), channel_id=1, source_target_pairs={{0,4},{2,6},{4,0},{6,2},{1,5},{3,7},{5,1},{7,3},{8,12},{10,14},{12... | collective-permute-start | bytes 786440 | tf_op jit(solution)/shard_map/ppermute | solution.py:266
  565.3 3.1 slice.66
  568.4 0.7 collective-permute-start.7
  569.1 3.1 slice.68
  572.5 46.9 %all-gather.10.cloned.1.call-done = bf16[2,256,4096]{2,1,0:T(8,128)(2,1)} async-done(((bf16[2,256,1024]{2,1,0:T(8,128)(2,1)}), bf16[2,256,4096]{2,1,0:T(8,128)(2,1)}) %all-gather.10.cloned.1.call-update) | async-done | bytes 4194320 | tf_op jit(solution)/shard_map/all_gather | solution.py:234
  619.4 5.9 fusion
  625.5 4.5 fusion.2
  630.6 4.6 fusion.4
  635.4 2.4 fusion.49
  637.8 2.3 fusion.50
  640.1 2.3 fusion.29
  642.4 2.5 fusion.30
  645.6 2.8 fusion.6
  648.4 2.8 fusion.24
  651.5 1.5 collective-permute-start.16
  653.2 1.5 collective-permute-start.10
  654.8 1.5 collective-permute-start.12
  656.4 1.5 collective-permute-start.14
  658.0 5.5 collective-permute-done.10
  663.5 5.5 collective-permute-done.12
  669.0 3.9 collective-permute-done.14
  673.1 1.3 copy-done.3
  (95 shorter events, 7.3 us)
Async XLA Ops:
  6.5 2.7 copy-start.1
  6.6 4.0 copy-start.5
  6.6 5.4 copy-start.4
  14.8 6.5 copy-start.2
  14.8 43.5 %all-to-all-start = ((bf16[4,768,256]{2,1,0:T(8,128)(2,1)}), bf16[4,768,256]{2,1,0:T(8,128)(2,1)}, u32[]{:S(2)}, u32[]{:S(2)}) async-start(bf16[4,768,256]{2,1,0:T(8,128)(2,1)} %maximum_bitcast_fusion), calls=%async_computation | async-start | bytes 3145728 | tf_op jit(solution)/shard_map/all_to_all | solution.py:292
  21.2 106.4 %all-gather.12.cloned.1.call-start = ((), (), s32[]{:S(2)}) async-start(), calls=%async_computation.5 | async-start | bytes 7864320 | tf_op jit(solution)/shard_map/all_gather | solution.py:295
  58.3 69.3 %all-to-all-start.1 = ((bf16[4,256,1024]{2,1,0:T(8,128)(2,1)}), bf16[4,256,1024]{2,1,0:T(8,128)(2,1)S(1)}, u32[]{:S(2)}, u32[]{:S(2)}) async-start(bf16[4,256,1024]{2,1,0:T(8,128)(2,1)} %bitcast.194), calls=%async_computation.1 | async-start | bytes 4194304 | tf_op jit(solution)/shard_map/all_to_all | solution.py:294
  62.0 465.8 %all-gather.6.cloned.1.call-start = ((), (), s32[]{:S(2)}) async-start(), calls=%async_computation.2 | async-start | bytes 2621440 | tf_op jit(solution)/shard_map/all_gather | solution.py:234
  127.6 1.3 copy-start
  210.9 321.0 %all-gather.8.cloned.1.call-start = ((), (), s32[]{:S(2)}) async-start(), calls=%async_computation.3 | async-start | bytes 2621440 | tf_op jit(solution)/shard_map/all_gather | solution.py:234
  316.2 303.2 %all-gather.10.cloned.1.call-start = ((), (), s32[]{:S(2)}) async-start(), calls=%async_computation.4 | async-start | bytes 5242880 | tf_op jit(solution)/shard_map/all_gather | solution.py:234
  316.5 219.6 %collective-permute-start.1 = (bf16[4096,512]{1,0:T(8,128)(2,1)}, bf16[4096,512]{1,0:T(8,128)(2,1)}, u32[]{:S(2)}, u32[]{:S(2)}) collective-permute-start(bf16[4096,512]{1,0:T(8,128)(2,1)} %param.9), channel_id=1, source_target_pairs={{0,2},{2,0},{4,6},{6,4},{1,3},{3,1},{5,7},{7,5},{8,10},{10,8},{12,... | collective-permute-start | bytes 12582920 | tf_op jit(solution)/shard_map/ppermute | solution.py:266
  318.0 225.4 %collective-permute-start.4 = (bf16[4096,512]{1,0:T(8,128)(2,1)}, bf16[4096,512]{1,0:T(8,128)(2,1)}, u32[]{:S(2)}, u32[]{:S(2)}) collective-permute-start(bf16[4096,512]{1,0:T(8,128)(2,1)} %param.9), channel_id=1, source_target_pairs={{0,4},{2,6},{4,0},{6,2},{1,5},{3,7},{5,1},{7,3},{8,12},{10,14},{12... | collective-permute-start | bytes 12582920 | tf_op jit(solution)/shard_map/ppermute | solution.py:266
  531.9 4.2 copy-start.9
  536.1 3.7 copy-start.7
  543.4 8.5 %collective-permute-start.2 = (bf16[256,512]{1,0:T(8,128)(2,1)S(1)}, bf16[256,512]{1,0:T(8,128)(2,1)S(1)}, u32[]{:S(2)}, u32[]{:S(2)}) collective-permute-start(bf16[256,512]{1,0:T(8,128)(2,1)S(1)} %fusion.88), channel_id=1, source_target_pairs={{0,1},{1,0},{2,3},{3,2},{4,5},{5,4},{6,7},{7,6},{8,9},{9,8},{10,11... | collective-permute-start | bytes 786440 | tf_op jit(solution)/shard_map/ppermute | solution.py:256
  551.1 2.4 collective-permute-start.5
  551.8 13.2 %collective-permute-start = (bf16[256,512]{1,0:T(8,128)(2,1)S(1)}, bf16[256,512]{1,0:T(8,128)(2,1)S(1)}, u32[]{:S(2)}, u32[]{:S(2)}) collective-permute-start(bf16[256,512]{1,0:T(8,128)(2,1)S(1)} %fusion.87), channel_id=1, source_target_pairs={{0,1},{1,0},{2,3},{3,2},{4,5},{5,4},{6,7},{7,6},{8,9},{9,8},{10,11... | collective-permute-start | bytes 786440 | tf_op jit(solution)/shard_map/ppermute | solution.py:256
  552.0 20.4 %collective-permute-start.3 = (bf16[256,512]{1,0:T(8,128)(2,1)S(1)}, bf16[256,512]{1,0:T(8,128)(2,1)S(1)}, u32[]{:S(2)}, u32[]{:S(2)}) collective-permute-start(bf16[256,512]{1,0:T(8,128)(2,1)S(1)} %fusion.68), channel_id=1, source_target_pairs={{0,2},{2,0},{4,6},{6,4},{1,3},{3,1},{5,7},{7,5},{8,10},{10,8},{12,... | collective-permute-start | bytes 786440 | tf_op jit(solution)/shard_map/ppermute | solution.py:266
  553.6 18.9 %collective-permute-start.6 = (bf16[256,512]{1,0:T(8,128)(2,1)S(1)}, bf16[256,512]{1,0:T(8,128)(2,1)S(1)}, u32[]{:S(2)}, u32[]{:S(2)}) collective-permute-start(bf16[256,512]{1,0:T(8,128)(2,1)S(1)} %fusion.62), channel_id=1, source_target_pairs={{0,4},{2,6},{4,0},{6,2},{1,5},{3,7},{5,1},{7,3},{8,12},{10,14},{12... | collective-permute-start | bytes 786440 | tf_op jit(solution)/shard_map/ppermute | solution.py:266
  568.4 71.8 %collective-permute-start.7 = (bf16[2048,512]{1,0:T(8,128)(2,1)}, bf16[2048,512]{1,0:T(8,128)(2,1)}, u32[]{:S(2)}, u32[]{:S(2)}) collective-permute-start(bf16[2048,512]{1,0:T(8,128)(2,1)} %slice.66), channel_id=1, source_target_pairs={{0,2},{2,0},{4,6},{6,4},{1,3},{3,1},{5,7},{7,5},{8,10},{10,8},{12,... | collective-permute-start | bytes 6291464 | tf_op jit(solution)/shard_map/ppermute | solution.py:266
  572.2 63.2 %collective-permute-start.8 = (bf16[2048,512]{1,0:T(8,128)(2,1)}, bf16[2048,512]{1,0:T(8,128)(2,1)}, u32[]{:S(2)}, u32[]{:S(2)}) collective-permute-start(bf16[2048,512]{1,0:T(8,128)(2,1)} %slice.68), channel_id=1, source_target_pairs={{0,4},{2,6},{4,0},{6,2},{1,5},{3,7},{5,1},{7,3},{8,12},{10,14},{12... | collective-permute-start | bytes 6291464 | tf_op jit(solution)/shard_map/ppermute | solution.py:266
  619.4 6.1 copy-start.6
  625.4 47.6 %collective-permute-start.17 = (bf16[256,512]{1,0:T(8,128)(2,1)S(1)}, bf16[256,512]{1,0:T(8,128)(2,1)S(1)}, u32[]{:S(2)}, u32[]{:S(2)}) collective-permute-start(bf16[256,512]{1,0:T(8,128)(2,1)S(1)} %fusion.82), channel_id=1, source_target_pairs={{0,1},{1,0},{2,3},{3,2},{4,5},{5,4},{6,7},{7,6},{8,9},{9,8},{10,11... | collective-permute-start | bytes 786440 | tf_op jit(solution)/shard_map/ppermute | solution.py:256
  630.0 5.4 copy-start.10
  630.1 21.4 %collective-permute-start.15 = (bf16[256,512]{1,0:T(8,128)(2,1)S(1)}, bf16[256,512]{1,0:T(8,128)(2,1)S(1)}, u32[]{:S(2)}, u32[]{:S(2)}) collective-permute-start(bf16[256,512]{1,0:T(8,128)(2,1)S(1)} %fusion.81), channel_id=1, source_target_pairs={{0,1},{1,0},{2,3},{3,2},{4,5},{5,4},{6,7},{7,6},{8,9},{9,8},{10,11... | collective-permute-start | bytes 786440 | tf_op jit(solution)/shard_map/ppermute | solution.py:256
  635.2 2.6 copy-start.8
  635.2 21.1 %collective-permute-start.13 = (bf16[256,512]{1,0:T(8,128)(2,1)S(1)}, bf16[256,512]{1,0:T(8,128)(2,1)S(1)}, u32[]{:S(2)}, u32[]{:S(2)}) collective-permute-start(bf16[256,512]{1,0:T(8,128)(2,1)S(1)} %fusion.80), channel_id=1, source_target_pairs={{0,1},{1,0},{2,3},{3,2},{4,5},{5,4},{6,7},{7,6},{8,9},{9,8},{10,11... | collective-permute-start | bytes 786440 | tf_op jit(solution)/shard_map/ppermute | solution.py:256
  645.1 8.0 %collective-permute-start.9 = (bf16[256,512]{1,0:T(8,128)(2,1)S(1)}, bf16[256,512]{1,0:T(8,128)(2,1)S(1)}, u32[]{:S(2)}, u32[]{:S(2)}) collective-permute-start(bf16[256,512]{1,0:T(8,128)(2,1)S(1)} %fusion.90), channel_id=1, source_target_pairs={{0,1},{1,0},{2,3},{3,2},{4,5},{5,4},{6,7},{7,6},{8,9},{9,8},{10,11... | collective-permute-start | bytes 786440 | tf_op jit(solution)/shard_map/ppermute | solution.py:256
  651.3 3.4 collective-permute-start.11
  651.5 21.4 %collective-permute-start.16 = (bf16[256,512]{1,0:T(8,128)(2,1)S(1)}, bf16[256,512]{1,0:T(8,128)(2,1)S(1)}, u32[]{:S(2)}, u32[]{:S(2)}) collective-permute-start(bf16[256,512]{1,0:T(8,128)(2,1)S(1)} %fusion.76), channel_id=1, source_target_pairs={{0,4},{2,6},{4,0},{6,2},{1,5},{3,7},{5,1},{7,3},{8,12},{10,14},{12... | collective-permute-start | bytes 786440 | tf_op jit(solution)/shard_map/ppermute | solution.py:266
  653.2 10.2 %collective-permute-start.10 = (bf16[256,512]{1,0:T(8,128)(2,1)S(1)}, bf16[256,512]{1,0:T(8,128)(2,1)S(1)}, u32[]{:S(2)}, u32[]{:S(2)}) collective-permute-start(bf16[256,512]{1,0:T(8,128)(2,1)S(1)} %fusion.56), channel_id=1, source_target_pairs={{0,6},{2,4},{4,2},{6,0},{1,7},{3,5},{5,3},{7,1},{8,14},{10,12},{12... | collective-permute-start | bytes 786440 | tf_op jit(solution)/shard_map/ppermute | solution.py:266
  654.8 14.2 %collective-permute-start.12 = (bf16[256,512]{1,0:T(8,128)(2,1)S(1)}, bf16[256,512]{1,0:T(8,128)(2,1)S(1)}, u32[]{:S(2)}, u32[]{:S(2)}) collective-permute-start(bf16[256,512]{1,0:T(8,128)(2,1)S(1)} %fusion.78), channel_id=1, source_target_pairs={{0,6},{2,4},{4,2},{6,0},{1,7},{3,5},{5,3},{7,1},{8,14},{10,12},{12... | collective-permute-start | bytes 786440 | tf_op jit(solution)/shard_map/ppermute | solution.py:266
  656.4 16.5 %collective-permute-start.14 = (bf16[256,512]{1,0:T(8,128)(2,1)S(1)}, bf16[256,512]{1,0:T(8,128)(2,1)S(1)}, u32[]{:S(2)}, u32[]{:S(2)}) collective-permute-start(bf16[256,512]{1,0:T(8,128)(2,1)S(1)} %fusion.77), channel_id=1, source_target_pairs={{0,2},{2,0},{4,6},{6,4},{1,3},{3,1},{5,7},{7,5},{8,10},{10,8},{12,... | collective-permute-start | bytes 786440 | tf_op jit(solution)/shard_map/ppermute | solution.py:266
  673.1 1.3 copy-start.3
Sparse Core Ops, SparseCore 0:
  58.4 69.1 all-gather.11
  211.0 51.3 all-gather.5
  316.4 57.0 all-gather.7
  527.8 91.5 all-gather.9

commit v3 on v2

--- a/solution.py
+++ b/solution.py
@@ -45,13 +45,14 @@
     return jnp.max(sums, axis=0, keepdims=True)
 
 
-def attend(queries, entries, lengths, j, start, stride, count):
+def attend(queries, key_parts, value_parts, ids, lengths, j, nj, start, stride, count):
     _, rows, width = queries.shape
-    nj, nz, local, pair = entries.shape
+    local, head = key_parts[0].shape[1:]
     cached = local - rows
-    head = pair // 2
+    pair = 2 * head
+    parts = len(key_parts)
     group = width // head
-    shards = nj * nz
+    shards = ids.shape[0]
     slots = lengths.shape[0]
     slot = cached * shards // slots
     per_shard = cached // slot
@@ -60,44 +61,58 @@
     span_blocks = span // block
     stack = group * rows
     slice_rows = min(stack, 512)
-    slow_rows = min(stack, 256)
+    slow_rows = min(stack, 128)
     scale = math.log2(math.e) / math.sqrt(head)
     capacity = span + shards * cached + block
 
-    def kernel(meta_ref, len_ref, q_ref, kv_ref, o_ref, keys, values, stacked, acc, top, norms, counts, bounds):
+    def kernel(meta_ref, len_ref, q_ref, *refs):
+        key_refs, value_refs = refs[:parts], refs[parts : 2 * parts]
+        o_ref, staged, keys, values, stacked, acc, top, norms, counts, bounds, arrived = refs[2 * parts :]
         step = pl.program_id(0)
 
         @pl.when(step == 0)
         def _():
             norms[...] = jnp.zeros_like(norms)
 
-            def put_span(shard, carry):
+            index = lax.broadcasted_iota(jnp.int32, (slot, head), 0)
+            copies = []
+            for which, pieces in enumerate((key_refs, value_refs)):
+                base = 0
+                for piece in pieces:
+                    size = piece.shape[0]
+                    copies.append(
+                        pltpu.make_async_copy(
+                            piece, staged.at[which, pl.ds(base, size)], arrived.at[len(copies)]
+                        )
+                    )
+                    base += size
+            for copy in copies:
+                copy.start()
+            for copy in copies:
+                copy.wait()
+
+            def put_shard(n, at):
+                shard = meta_ref[2 + n]
                 place = pl.ds(pl.multiple_of(shard * rows, rows), rows)
-                piece = kv_ref[shard % nj, shard // nj, cached:, :]
-                keys[place, :] = piece[:, :head]
-                values[place, :head] = piece[:, head:]
+                piece = staged[0, n, cached:, :]
+                keys[place, :] = piece
+                values[place, :head] = staged[1, n, cached:, :]
                 values[place, head:] = jnp.ones((rows, head), BF16)
-                norms[...] = jnp.maximum(norms[...], square_bound(piece[:, :head]))
-                return carry
-
-            lax.fori_loop(0, shards, put_span, 0)
-            index = lax.broadcasted_iota(jnp.int32, (slot, head), 0)
-
-            def put_slot(number, at):
-                shard = number // per_shard
-                inside = pl.multiple_of((number % per_shard) * slot, slot)
-                piece = kv_ref[shard % nj, shard // nj, pl.ds(inside, slot), :]
-                size = len_ref[number]
-                place = pl.ds(pl.multiple_of(at, 16), slot)
-                keys[place, :] = piece[:, :head]
-                values[place, :head] = piece[:, head:]
-                values[place, head:] = jnp.where(index < size, 1.0, 0.0).astype(BF16)
-                norms[...] = jnp.maximum(norms[...], square_bound(piece[:, :head]))
-                return at + (size + 15) // 16 * 16
-
-            end = lax.fori_loop(0, slots, put_slot, span)
+                norms[...] = jnp.maximum(norms[...], square_bound(piece))
+                for k in range(per_shard):
+                    piece = staged[0, n, k * slot : (k + 1) * slot, :]
+                    size = len_ref[shard * per_shard + k]
+                    place = pl.ds(pl.multiple_of(at, 16), slot)
+                    keys[place, :] = piece
+                    values[place, :head] = staged[1, n, k * slot : (k + 1) * slot, :]
+                    values[place, head:] = jnp.where(index < size, 1.0, 0.0).astype(BF16)
+                    norms[...] = jnp.maximum(norms[...], square_bound(piece))
+                    at = at + (size + 15) // 16 * 16
+                return at
+
+            end = lax.fori_loop(0, shards, put_shard, jnp.int32(span))
             place = pl.ds(pl.multiple_of(end, 16), block)
-            keys[place, :] = jnp.broadcast_to(kv_ref[0, 0, 0:1, :head], (block, head))
+            keys[place, :] = jnp.broadcast_to(staged[0, 0, 0:1, :], (block, head))
             values[place, :] = jnp.zeros((block, pair), BF16)
             counts[0] = (end - span + block - 1) // block
             bounds[0] = jnp.max(norms[...])
@@ -189,15 +204,17 @@
             part = slice(g * rows, (g + 1) * rows)
             o_ref[0, :, g * head : (g + 1) * head] = (acc[part, :head] / acc[part, head:]).astype(BF16)
 
+    meta = jnp.concatenate([jnp.stack([j, jnp.int32(start)]).astype(jnp.int32), ids])
     grid_spec = pltpu.PrefetchScalarGridSpec(
         num_scalar_prefetch=2,
         grid=(count,),
         in_specs=[
             pl.BlockSpec((1, rows, width), lambda i, meta, size: (meta[1] + i * stride, 0, 0)),
-            pl.BlockSpec(memory_space=pltpu.VMEM),
-        ],
+        ]
+        + [pl.BlockSpec(memory_space=pl.ANY)] * (2 * parts),
         out_specs=pl.BlockSpec((1, rows, width), lambda i, meta, size: (i, 0, 0)),
         scratch_shapes=[
+            pltpu.VMEM((2, shards, local, head), BF16),
             pltpu.VMEM((capacity, head), BF16),
             pltpu.VMEM((capacity, pair), BF16),
             pltpu.VMEM((stack, head), BF16),
@@ -206,6 +223,7 @@
             pltpu.VMEM((1, head), F32),
             pltpu.SMEM((1,), jnp.int32),
             pltpu.SMEM((1,), F32),
+            pltpu.SemaphoreType.DMA((2 * parts,)),
         ],
     )
     return pl.pallas_call(
@@ -214,23 +232,23 @@
         out_shape=jax.ShapeDtypeStruct((count, rows, width), BF16),
         compiler_params=pltpu.CompilerParams(vmem_limit_bytes=60 << 20),
         name="attend",
-    )(jnp.stack([j, jnp.int32(start)]).astype(jnp.int32), lengths, queries, entries)
-
-
-def project(rotated, entries, lengths, out_weight, j, nz, nt):
-    nj = entries.shape[0]
+    )(meta, lengths, queries, *key_parts, *value_parts)
+
+
+def project(rotated, key_parts, value_parts, ids, lengths, out_weight, j, nz, nj, nt):
     groups = nz // nt
     rows, columns = rotated.shape[1], out_weight.shape[1]
     half = out_weight.shape[0] // 2
     tp = lax.axis_index("tp")
-    entries, out_weight = lax.optimization_barrier((entries, out_weight))
+    key_parts, value_parts, out_weight = lax.optimization_barrier((key_parts, value_parts, out_weight))
     near = move(1, out_weight)
     far = move(2, out_weight)
     pieces = []
     for g in range(groups):
         calls = [(owner, 1) for owner in reversed(range(nt))] if g < groups - 1 else [(0, nt)]
         for owner, count in calls:
-            part = attend(rotated, entries, lengths, j, owner * groups + g, groups, count)
+            first = owner * groups + g
+            part = attend(rotated, key_parts, value_parts, ids, lengths, j, nj, first, groups, count)
             pieces.append(lax.all_gather(part, "z", axis=2, tiled=True))
     across = (move(1, far[:half]), move(2, near[half:]))
     weights = [(out_weight,), (near,), (far,), across]
@@ -262,6 +280,12 @@
     return out.reshape(groups * nj * rows, columns)
 
 
+def spread(own):
+    half = own.shape[0] // 2
+    near, far = move(1, own), move(2, own)
+    return [own, near, far, move(1, far[:half]), move(2, near[half:])]
+
+
 def move(r, array):
     return lax.ppermute(array, "j", [(i, i ^ r) for i in range(4)])
 
@@ -287,16 +311,23 @@
     local = jnp.concatenate([cache, span], axis=0).transpose(1, 0, 2)
     rotated = rotate(queries.reshape(rows, width // head, head).astype(F32), positions)
     rotated = rotated.astype(BF16).reshape(rows, kv_local, width // kv_local).transpose(1, 0, 2)
-    split = nz % nt == 0 and nj == 4
+    split = nz % nt == 0 and nj == 4 and nz % 2 == 0
+    keys, values = local[..., :head], local[..., head:]
     if nz > 1:
-        local = lax.all_to_all(local, "z", 0, 0, tiled=True)
-        rotated, local = lax.optimization_barrier((rotated, local))
+        keys = lax.all_to_all(keys, "z", 0, 0, tiled=True)
+        values, keys = lax.optimization_barrier((values, keys))
+        values = lax.all_to_all(values, "z", 0, 0, tiled=True)
+        rotated, values = lax.optimization_barrier((rotated, values))
         rotated = lax.all_to_all(rotated, "z", 0, 0, tiled=True)
-    entries = lax.all_gather(local, "j", axis=0, tiled=False)
-
+    every = jnp.arange(nz, dtype=jnp.int32) * nj
     if split:
-        return project(rotated, entries, lengths, out_weight, j, nz, nt)
-    attention = attend(rotated, entries, lengths, j, 0, 1, nz)
+        ids = jnp.concatenate([every + j, every + (j ^ 1), every + (j ^ 2), every + (j ^ 3)]).astype(jnp.int32)
+        key_parts, value_parts = spread(keys), spread(values)
+        return project(rotated, key_parts, value_parts, ids, lengths, out_weight, j, nz, nj, nt)
+    ids = (jnp.arange(nj, dtype=jnp.int32)[:, None] + every[None, :]).reshape(-1)
+    key_parts = [lax.all_gather(keys, "j", axis=0, tiled=True)]
+    value_parts = [lax.all_gather(values, "j", axis=0, tiled=True)]
+    attention = attend(rotated, key_parts, value_parts, ids, lengths, j, nj, 0, 1, nz)
     wide = attention.reshape(nz * rows, -1)
     wide = lax.all_gather(wide, ("z", "j"), axis=0, tiled=True)
     projected = jnp.dot(wide, out_weight, preferred_element_type=F32).astype(BF16)

time: 682 us -> 866 us (1.27)
  Pallas kernels: 384 us -> 576 us
  waiting for transfers between devices: 156 us -> 90.9 us
  blocking collectives: 0 us -> 26.2 us
  starting transfers between devices: 46 us -> 65.6 us
  local copies, waits for them, and re-layouts: 19 us -> 30.6 us
    pallas_call x3, Pallas kernels: 384 us -> 576 us  [attend(): pl.pallas_call(kernel, grid_spec=grid_spec, out_shape=jax.ShapeDtypeStruc...]
    ppermute x10 -> x18, waiting for transfers between devices: 14.9 us -> 81.9 us  [move(): return lax.ppermute(array, 'j', [(i, i ^ r) for i in range(4)])]
    all_gather x1 -> x0, waiting for transfers between devices: 65 us -> none  [body(): entries = lax.all_gather(local, 'j', axis=0, tiled=False)]
    all_gather x3, waiting for transfers between devices: 46.9 us -> 2.37 us  [project(): pieces.append(lax.all_gather(part, 'z', axis=2, tiled=True))]
    all_to_all x0 -> x1, blocking collectives: none -> 26.2 us  [body(): keys = lax.all_to_all(keys, 'z', 0, 0, tiled=True)]
    ppermute x10 -> x18, starting transfers between devices: 33.4 us -> 56.3 us  [move(): return lax.ppermute(array, 'j', [(i, i ^ r) for i in range(4)])]
    all_to_all x1, waiting for transfers between devices: 28.7 us -> 6.58 us  [body(): values = lax.all_to_all(values, 'z', 0, 0, tiled=True)]
  transfers between devices with their start and end apart: 24 -> 31, of which waited for: 6 -> 11; matrix products, arithmetic and copies ran while one was open for 10% -> 8% of each run, Pallas kernels for 44% -> 53%
where the time goes in v3:
time: 866 us; the launch traced here: 865 us
  Pallas kernels  576 us (67%)
  waiting for transfers between devices  90.9 us (10%)
  starting transfers between devices  65.6 us (8%)
  matrix products  53 us (6%)
  local copies, waits for them, and re-layouts  30.6 us (4%)
  blocking collectives  26.2 us (3%)
  between operations  14.4 us (2%)
    pallas_call x3, Pallas kernels, attend(): pl.pallas_call(kernel, grid_spec=grid_spec, out_shape=jax.ShapeDtypeStruc...  576 us
    ppermute x18, waiting for transfers between devices, move(): return lax.ppermute(array, 'j', [(i, i ^ r) for i in range(4)])  81.9 us
    ppermute x18, starting transfers between devices, move(): return lax.ppermute(array, 'j', [(i, i ^ r) for i in range(4)])  56.3 us
    dot_general x9, matrix products, times(): jnp.einsum('ctk,kn->ctn', left, weights[r][0], preferred_element_type=F32)  37.8 us
    all_to_all x1, blocking collectives, body(): keys = lax.all_to_all(keys, 'z', 0, 0, tiled=True)  26.2 us
  transfers between devices with their start and end apart: 31, of which 11 were waited for; matrix products, arithmetic and copies ran while one was open for 8% of the time, Pallas kernels for 53%

profile of v3, /device:TPU:0, one launch (start us, length us, event | category | flops | bytes accessed | tf_op | source)
XLA Modules:
  0.0 864.6 jit_solution(2669133374166084124)
XLA Ops:
  6.6 2.6 reshape.140
  14.8 26.2 %all_to_all.15.refs_0_ = bf16[4,768,128]{2,1,0:T(8,128)(2,1)S(1)} all-to-all(bf16[4,768,128]{2,1,0:T(8,128)(2,1)S(1)} %get-tuple-element.37), channel_id=1, replica_groups=mesh['z'=4,'j'=4,'tp'=2] {'z'}, dimensions={0} | all-to-all | bytes 1572864 | tf_op jit(solution)/shard_map/all_to_all | solution.py:317
  41.0 3.5 all-to-all-start.1
  44.5 4.3 copy.19
  48.8 2.9 subtract_convert_fusion
  51.7 1.5 pad_maximum_fusion
  53.2 4.0 copy.20
  57.2 6.6 all-to-all-done.1.refs_5_
  64.7 3.6 all-to-all-start.2
  68.3 1.6 collective-permute-start.1
  72.4 16.4 %collective-permute-done.1.refs_2_ = bf16[4,768,128]{2,1,0:T(8,128)(2,1)S(1)} collective-permute-done((bf16[4,768,128]{2,1,0:T(8,128)(2,1)S(1)}, bf16[4,768,128]{2,1,0:T(8,128)(2,1)S(1)}, u32[]{:S(2)}, u32[]{:S(2)}) %collective-permute-start.1) | collective-permute-done | bytes 786464 | tf_op jit(solution)/shard_map/ppermute | solution.py:290
  92.2 1.5 collective-permute-start.3
  93.7 11.9 %collective-permute-done.5.refs_7_ = bf16[4,768,128]{2,1,0:T(8,128)(2,1)S(1)} collective-permute-done((bf16[4,768,128]{2,1,0:T(8,128)(2,1)}, bf16[4,768,128]{2,1,0:T(8,128)(2,1)S(1)}, u32[]{:S(2)}, u32[]{:S(2)}) %collective-permute-start.5) | collective-permute-done | bytes 786464 | tf_op jit(solution)/shard_map/ppermute | solution.py:290
  110.5 1.5 collective-permute-start.7
  112.7 2.9 collective-permute-done.2.refs_3_
  115.6 6.3 collective-permute-done.6.refs_8_
  124.0 119.3 %attend.3 = bf16[1,256,1024]{2,1,0:T(8,128)(2,1)} custom-call(s32[18]{0:T(128)} %concatenate.38.meta_ref, s32[32]{0:T(128)} %len_ref.5, bf16[4,256,1024]{2,1,0:T(8,128)(2,1)} %copy-done, bf16[4,768,128]{2,1,0:T(8,128)(2,1)} %copy-done.1, bf16[4,768,128]{2,1,0:T(8,128)(2,1)} %copy-done.4, bf16[4,768,128]{2,1,0:T(8,128)(2,1)} %copy-done.3, ...), custom_call_target="tpu_custom_call" | custom-call | tf_op jit(solution)/shard_map/attend/pallas_call | solution.py:229
  243.4 9.6 %collective-permute-start.12 = (bf16[4096,512]{1,0:T(8,128)(2,1)}, bf16[4096,512]{1,0:T(8,128)(2,1)}, u32[]{:S(2)}, u32[]{:S(2)}) collective-permute-start(bf16[4096,512]{1,0:T(8,128)(2,1)} %param.9), channel_id=1, source_target_pairs={{0,4},{2,6},{4,0},{6,2},{1,5},{3,7},{5,1},{7,3},{8,12},{10,14},{12... | collective-permute-start | bytes 12582920 | tf_op jit(solution)/shard_map/ppermute | solution.py:290
  253.0 1.5 collective-permute-start.9
  255.2 155.8 %attend.4 = bf16[1,256,1024]{2,1,0:T(8,128)(2,1)} custom-call(s32[18]{0:T(128)} %concatenate.42.meta_ref, s32[32]{0:T(128)} %len_ref.5, bf16[4,256,1024]{2,1,0:T(8,128)(2,1)} %copy-done, bf16[4,768,128]{2,1,0:T(8,128)(2,1)} %copy-done.1, bf16[4,768,128]{2,1,0:T(8,128)(2,1)} %copy-done.4, bf16[4,768,128]{2,1,0:T(8,128)(2,1)} %copy-done.3, ...), custom_call_target="tpu_custom_call" | custom-call | tf_op jit(solution)/shard_map/attend/pallas_call | solution.py:229
  411.7 301.1 %attend.5 = bf16[2,256,1024]{2,1,0:T(8,128)(2,1)} custom-call(s32[18]{0:T(128)} %concatenate.47.meta_ref, s32[32]{0:T(128)} %len_ref.5, bf16[4,256,1024]{2,1,0:T(8,128)(2,1)} %copy-done, bf16[4,768,128]{2,1,0:T(8,128)(2,1)} %copy-done.1, bf16[4,768,128]{2,1,0:T(8,128)(2,1)} %copy-done.4, bf16[4,768,128]{2,1,0:T(8,128)(2,1)} %copy-done.3, ...), custom_call_target="tpu_custom_call" | custom-call | tf_op jit(solution)/shard_map/attend/pallas_call | solution.py:229
  712.8 1.7 slice.96
  715.0 3.0 slice.98
  718.1 27.2 %collective-permute-start.16 = (bf16[2048,512]{1,0:T(8,128)(2,1)}, bf16[2048,512]{1,0:T(8,128)(2,1)}, u32[]{:S(2)}, u32[]{:S(2)}) collective-permute-start(bf16[2048,512]{1,0:T(8,128)(2,1)} %slice.98), channel_id=1, source_target_pairs={{0,4},{2,6},{4,0},{6,2},{1,5},{3,7},{5,1},{7,3},{8,12},{10,14},{12... | collective-permute-start | bytes 6291464 | tf_op jit(solution)/shard_map/ppermute | solution.py:290
  745.2 4.6 fusion.31
  749.8 4.2 fusion.40
  754.2 3.6 fusion.46
  757.9 3.5 fusion.37
  761.9 3.5 fusion.43
  765.4 3.5 fusion.34
  769.5 22.1 %collective-permute-done.16 = bf16[2048,512]{1,0:T(8,128)(2,1)} collective-permute-done((bf16[2048,512]{1,0:T(8,128)(2,1)}, bf16[2048,512]{1,0:T(8,128)(2,1)}, u32[]{:S(2)}, u32[]{:S(2)}) %collective-permute-start.16) | collective-permute-done | bytes 2097184 | tf_op jit(solution)/shard_map/ppermute | solution.py:290
  791.6 2.3 fusion.49
  794.0 2.3 fusion.29
  796.3 2.3 fusion.50
  798.7 2.3 fusion.30
  801.4 1.5 collective-permute-start.11
  803.4 2.2 collective-permute-start.18
  805.6 5.0 collective-permute-done.11
  810.7 6.2 collective-permute-done.18
  816.9 2.3 all-gather.8.cloned.1.call-done
  819.3 5.9 fusion
  825.3 4.5 fusion.4
  830.5 3.0 fusion.6
  833.5 2.8 fusion.24
  836.5 4.5 fusion.2
  841.7 2.4 collective-permute-start.20
  845.5 6.3 collective-permute-done.20
  851.9 4.7 collective-permute-done.22
  (127 shorter events, 27.7 us)
Async XLA Ops:
  6.5 2.7 copy-start.7
  6.6 4.0 copy-start.13
  6.6 5.4 copy-start.12
  41.0 28.9 %copy-start.1 = (bf16[4,768,128]{2,1,0:T(8,128)(2,1)}, bf16[4,768,128]{2,1,0:T(8,128)(2,1)S(1)}, u32[]{:S(2)}) copy-start(bf16[4,768,128]{2,1,0:T(8,128)(2,1)S(1)} %all_to_all.15.refs_0_) | copy-start | bytes 2359300
  41.0 22.8 %all-to-all-start.1 = ((bf16[4,768,128]{2,1,0:T(8,128)(2,1)}), bf16[4,768,128]{2,1,0:T(8,128)(2,1)S(1)}, u32[]{:S(2)}, u32[]{:S(2)}) async-start(bf16[4,768,128]{2,1,0:T(8,128)(2,1)} %get-tuple-element.20), calls=%async_computation.1 | async-start | bytes 1572864 | tf_op jit(solution)/shard_map/all_to_all | solution.py:319
  63.8 0.9 copy-start.2
  64.7 57.2 %all-to-all-start.2 = ((bf16[4,256,1024]{2,1,0:T(8,128)(2,1)}), bf16[4,256,1024]{2,1,0:T(8,128)(2,1)S(1)}, u32[]{:S(2)}, u32[]{:S(2)}) async-start(bf16[4,256,1024]{2,1,0:T(8,128)(2,1)} %bitcast.189), calls=%async_computation.2 | async-start | bytes 4194304 | tf_op jit(solution)/shard_map/all_to_all | solution.py:321
  68.3 676.9 %all-gather.4.cloned.1.call-start = ((), (), s32[]{:S(2)}) async-start(), calls=%async_computation.3 | async-start | bytes 2621440 | tf_op jit(solution)/shard_map/all_gather | solution.py:252
  68.3 20.5 %collective-permute-start.1 = (bf16[4,768,128]{2,1,0:T(8,128)(2,1)S(1)}, bf16[4,768,128]{2,1,0:T(8,128)(2,1)S(1)}, u32[]{:S(2)}, u32[]{:S(2)}) collective-permute-start(bf16[4,768,128]{2,1,0:T(8,128)(2,1)S(1)} %all_to_all.15.refs_0_), channel_id=1, source_target_pairs={{0,4},{2,6},{4,0},{6,2},{1,5},{3,7},{5,1},{7,3},{8,12},{10,14},{12... | collective-permute-start | bytes 2359304 | tf_op jit(solution)/shard_map/ppermute | solution.py:290
  69.9 21.2 %collective-permute-start = (bf16[4,768,128]{2,1,0:T(8,128)(2,1)S(1)}, bf16[4,768,128]{2,1,0:T(8,128)(2,1)S(1)}, u32[]{:S(2)}, u32[]{:S(2)}) collective-permute-start(bf16[4,768,128]{2,1,0:T(8,128)(2,1)S(1)} %all_to_all.15.refs_0_), channel_id=1, source_target_pairs={{0,2},{2,0},{4,6},{6,4},{1,3},{3,1},{5,7},{7,5},{8,10},{10,8},{12,... | collective-permute-start | bytes 2359304 | tf_op jit(solution)/shard_map/ppermute | solution.py:290
  71.4 34.3 %collective-permute-start.5 = (bf16[4,768,128]{2,1,0:T(8,128)(2,1)}, bf16[4,768,128]{2,1,0:T(8,128)(2,1)S(1)}, u32[]{:S(2)}, u32[]{:S(2)}) collective-permute-start(bf16[4,768,128]{2,1,0:T(8,128)(2,1)} %copy-done.2), channel_id=1, source_target_pairs={{0,4},{2,6},{4,0},{6,2},{1,5},{3,7},{5,1},{7,3},{8,12},{10,14},{12... | collective-permute-start | bytes 2359304 | tf_op jit(solution)/shard_map/ppermute | solution.py:290
  71.9 36.9 %collective-permute-start.4 = (bf16[4,768,128]{2,1,0:T(8,128)(2,1)}, bf16[4,768,128]{2,1,0:T(8,128)(2,1)S(1)}, u32[]{:S(2)}, u32[]{:S(2)}) collective-permute-start(bf16[4,768,128]{2,1,0:T(8,128)(2,1)} %copy-done.2), channel_id=1, source_target_pairs={{0,2},{2,0},{4,6},{6,4},{1,3},{3,1},{5,7},{7,5},{8,10},{10,8},{12,... | collective-permute-start | bytes 2359304 | tf_op jit(solution)/shard_map/ppermute | solution.py:290
  88.8 2.3 copy-start.3
  89.6 26.0 %collective-permute-start.2 = (bf16[2,768,128]{2,1,0:T(8,128)(2,1)}, bf16[2,768,128]{2,1,0:T(8,128)(2,1)S(1)}, u32[]{:S(2)}, u32[]{:S(2)}) collective-permute-start(bf16[2,768,128]{2,1,0:T(8,128)(2,1)} %slice.91), channel_id=1, source_target_pairs={{0,2},{2,0},{4,6},{6,4},{1,3},{3,1},{5,7},{7,5},{8,10},{10,8},{12,... | collective-permute-start | bytes 1179656 | tf_op jit(solution)/shard_map/ppermute | solution.py:290
  91.1 1.1 copy-start.4
  92.2 23.4 %collective-permute-start.3 = (bf16[2,768,128]{2,1,0:T(8,128)(2,1)}, bf16[2,768,128]{2,1,0:T(8,128)(2,1)S(1)}, u32[]{:S(2)}, u32[]{:S(2)}) collective-permute-start(bf16[2,768,128]{2,1,0:T(8,128)(2,1)} %slice.92), channel_id=1, source_target_pairs={{0,4},{2,6},{4,0},{6,2},{1,5},{3,7},{5,1},{7,3},{8,12},{10,14},{12... | collective-permute-start | bytes 1179656 | tf_op jit(solution)/shard_map/ppermute | solution.py:290
  105.7 0.9 copy-start.5
  107.3 14.6 %collective-permute-start.6 = (bf16[2,768,128]{2,1,0:T(8,128)(2,1)}, bf16[2,768,128]{2,1,0:T(8,128)(2,1)S(1)}, u32[]{:S(2)}, u32[]{:S(2)}) collective-permute-start(bf16[2,768,128]{2,1,0:T(8,128)(2,1)} %slice.93), channel_id=1, source_target_pairs={{0,2},{2,0},{4,6},{6,4},{1,3},{3,1},{5,7},{7,5},{8,10},{10,8},{12,... | collective-permute-start | bytes 1179656 | tf_op jit(solution)/shard_map/ppermute | solution.py:290
  108.8 0.9 copy-start.6
  110.5 11.4 %collective-permute-start.7 = (bf16[2,768,128]{2,1,0:T(8,128)(2,1)}, bf16[2,768,128]{2,1,0:T(8,128)(2,1)}, u32[]{:S(2)}, u32[]{:S(2)}) collective-permute-start(bf16[2,768,128]{2,1,0:T(8,128)(2,1)} %slice.94), channel_id=1, source_target_pairs={{0,4},{2,6},{4,0},{6,2},{1,5},{3,7},{5,1},{7,3},{8,12},{10,14},{12... | collective-permute-start | bytes 1179656 | tf_op jit(solution)/shard_map/ppermute | solution.py:290
  115.6 6.3 copy-start.8
  115.6 6.3 copy-start.9
  121.9 0.8 copy-start.10
  122.7 1.3 copy-start
  243.4 506.4 %all-gather.6.cloned.1.call-start = ((), (), s32[]{:S(2)}) async-start(), calls=%async_computation.4 | async-start | bytes 2621440 | tf_op jit(solution)/shard_map/all_gather | solution.py:252
  243.4 469.4 %collective-permute-start.12 = (bf16[4096,512]{1,0:T(8,128)(2,1)}, bf16[4096,512]{1,0:T(8,128)(2,1)}, u32[]{:S(2)}, u32[]{:S(2)}) collective-permute-start(bf16[4096,512]{1,0:T(8,128)(2,1)} %param.9), channel_id=1, source_target_pairs={{0,4},{2,6},{4,0},{6,2},{1,5},{3,7},{5,1},{7,3},{8,12},{10,14},{12... | collective-permute-start | bytes 12582920 | tf_op jit(solution)/shard_map/ppermute | solution.py:290
  253.0 462.0 %collective-permute-start.9 = (bf16[4096,512]{1,0:T(8,128)(2,1)}, bf16[4096,512]{1,0:T(8,128)(2,1)}, u32[]{:S(2)}, u32[]{:S(2)}) collective-permute-start(bf16[4096,512]{1,0:T(8,128)(2,1)} %param.9), channel_id=1, source_target_pairs={{0,2},{2,0},{4,6},{6,4},{1,3},{3,1},{5,7},{7,5},{8,10},{10,8},{12,... | collective-permute-start | bytes 12582920 | tf_op jit(solution)/shard_map/ppermute | solution.py:290
  411.0 408.3 %all-gather.8.cloned.1.call-start = ((), (), s32[]{:S(2)}) async-start(), calls=%async_computation.5 | async-start | bytes 5242880 | tf_op jit(solution)/shard_map/all_gather | solution.py:252
  714.6 79.4 %collective-permute-start.15 = (bf16[2048,512]{1,0:T(8,128)(2,1)S(1)}, bf16[2048,512]{1,0:T(8,128)(2,1)}, u32[]{:S(2)}, u32[]{:S(2)}) collective-permute-start(bf16[2048,512]{1,0:T(8,128)(2,1)S(1)} %slice.96), channel_id=1, source_target_pairs={{0,2},{2,0},{4,6},{6,4},{1,3},{3,1},{5,7},{7,5},{8,10},{10,8},{12,... | collective-permute-start | bytes 6291464 | tf_op jit(solution)/shard_map/ppermute | solution.py:290
  718.1 73.6 %collective-permute-start.16 = (bf16[2048,512]{1,0:T(8,128)(2,1)}, bf16[2048,512]{1,0:T(8,128)(2,1)}, u32[]{:S(2)}, u32[]{:S(2)}) collective-permute-start(bf16[2048,512]{1,0:T(8,128)(2,1)} %slice.98), channel_id=1, source_target_pairs={{0,4},{2,6},{4,0},{6,2},{1,5},{3,7},{5,1},{7,3},{8,12},{10,14},{12... | collective-permute-start | bytes 6291464 | tf_op jit(solution)/shard_map/ppermute | solution.py:290
  749.8 4.4 copy-start.16
  754.1 3.7 copy-start.15
  754.1 48.7 %collective-permute-start.8 = (bf16[256,512]{1,0:T(8,128)(2,1)S(1)}, bf16[256,512]{1,0:T(8,128)(2,1)S(1)}, u32[]{:S(2)}, u32[]{:S(2)}) collective-permute-start(bf16[256,512]{1,0:T(8,128)(2,1)S(1)} %fusion.87), channel_id=1, source_target_pairs={{0,1},{1,0},{2,3},{3,2},{4,5},{5,4},{6,7},{7,6},{8,9},{9,8},{10,11... | collective-permute-start | bytes 786440 | tf_op jit(solution)/shard_map/ppermute | solution.py:274
  761.5 7.8 collective-permute-start.13
  769.0 32.2 %collective-permute-start.10 = (bf16[256,512]{1,0:T(8,128)(2,1)S(1)}, bf16[256,512]{1,0:T(8,128)(2,1)S(1)}, u32[]{:S(2)}, u32[]{:S(2)}) collective-permute-start(bf16[256,512]{1,0:T(8,128)(2,1)S(1)} %fusion.88), channel_id=1, source_target_pairs={{0,1},{1,0},{2,3},{3,2},{4,5},{5,4},{6,7},{7,6},{8,9},{9,8},{10,11... | collective-permute-start | bytes 786440 | tf_op jit(solution)/shard_map/ppermute | solution.py:274
  769.4 41.2 %collective-permute-start.14 = (bf16[256,512]{1,0:T(8,128)(2,1)S(1)}, bf16[256,512]{1,0:T(8,128)(2,1)S(1)}, u32[]{:S(2)}, u32[]{:S(2)}) collective-permute-start(bf16[256,512]{1,0:T(8,128)(2,1)S(1)} %fusion.62), channel_id=1, source_target_pairs={{0,4},{2,6},{4,0},{6,2},{1,5},{3,7},{5,1},{7,3},{8,12},{10,14},{12... | collective-permute-start | bytes 786440 | tf_op jit(solution)/shard_map/ppermute | solution.py:290
  801.1 2.1 collective-permute-start.17
  801.4 9.2 %collective-permute-start.11 = (bf16[256,512]{1,0:T(8,128)(2,1)S(1)}, bf16[256,512]{1,0:T(8,128)(2,1)S(1)}, u32[]{:S(2)}, u32[]{:S(2)}) collective-permute-start(bf16[256,512]{1,0:T(8,128)(2,1)S(1)} %fusion.68), channel_id=1, source_target_pairs={{0,2},{2,0},{4,6},{6,4},{1,3},{3,1},{5,7},{7,5},{8,10},{10,8},{12,... | collective-permute-start | bytes 786440 | tf_op jit(solution)/shard_map/ppermute | solution.py:290
  803.4 13.5 %collective-permute-start.18 = (bf16[256,512]{1,0:T(8,128)(2,1)S(1)}, bf16[256,512]{1,0:T(8,128)(2,1)S(1)}, u32[]{:S(2)}, u32[]{:S(2)}) collective-permute-start(bf16[256,512]{1,0:T(8,128)(2,1)S(1)} %fusion.56), channel_id=1, source_target_pairs={{0,6},{2,4},{4,2},{6,0},{1,7},{3,5},{5,3},{7,1},{8,14},{10,12},{12... | collective-permute-start | bytes 786440 | tf_op jit(solution)/shard_map/ppermute | solution.py:290
  819.3 6.1 copy-start.14
  825.2 31.4 %collective-permute-start.25 = (bf16[256,512]{1,0:T(8,128)(2,1)S(1)}, bf16[256,512]{1,0:T(8,128)(2,1)S(1)}, u32[]{:S(2)}, u32[]{:S(2)}) collective-permute-start(bf16[256,512]{1,0:T(8,128)(2,1)S(1)} %fusion.82), channel_id=1, source_target_pairs={{0,1},{1,0},{2,3},{3,2},{4,5},{5,4},{6,7},{7,6},{8,9},{9,8},{10,11... | collective-permute-start | bytes 786440 | tf_op jit(solution)/shard_map/ppermute | solution.py:274
  829.9 14.2 %collective-permute-start.21 = (bf16[256,512]{1,0:T(8,128)(2,1)S(1)}, bf16[256,512]{1,0:T(8,128)(2,1)S(1)}, u32[]{:S(2)}, u32[]{:S(2)}) collective-permute-start(bf16[256,512]{1,0:T(8,128)(2,1)S(1)} %fusion.80), channel_id=1, source_target_pairs={{0,1},{1,0},{2,3},{3,2},{4,5},{5,4},{6,7},{7,6},{8,9},{9,8},{10,11... | collective-permute-start | bytes 786440 | tf_op jit(solution)/shard_map/ppermute | solution.py:274
  836.4 5.2 collective-permute-start.19
  841.0 3.8 collective-permute-start.23
  841.7 10.2 %collective-permute-start.20 = (bf16[256,512]{1,0:T(8,128)(2,1)S(1)}, bf16[256,512]{1,0:T(8,128)(2,1)S(1)}, u32[]{:S(2)}, u32[]{:S(2)}) collective-permute-start(bf16[256,512]{1,0:T(8,128)(2,1)S(1)} %fusion.78), channel_id=1, source_target_pairs={{0,6},{2,4},{4,2},{6,0},{1,7},{3,5},{5,3},{7,1},{8,14},{10,12},{12... | collective-permute-start | bytes 786440 | tf_op jit(solution)/shard_map/ppermute | solution.py:290
  844.2 12.4 %collective-permute-start.22 = (bf16[256,512]{1,0:T(8,128)(2,1)S(1)}, bf16[256,512]{1,0:T(8,128)(2,1)S(1)}, u32[]{:S(2)}, u32[]{:S(2)}) collective-permute-start(bf16[256,512]{1,0:T(8,128)(2,1)S(1)} %fusion.77), channel_id=1, source_target_pairs={{0,2},{2,0},{4,6},{6,4},{1,3},{3,1},{5,7},{7,5},{8,10},{10,8},{12,... | collective-permute-start | bytes 786440 | tf_op jit(solution)/shard_map/ppermute | solution.py:290
  844.9 11.7 %collective-permute-start.24 = (bf16[256,512]{1,0:T(8,128)(2,1)S(1)}, bf16[256,512]{1,0:T(8,128)(2,1)S(1)}, u32[]{:S(2)}, u32[]{:S(2)}) collective-permute-start(bf16[256,512]{1,0:T(8,128)(2,1)S(1)} %fusion.76), channel_id=1, source_target_pairs={{0,4},{2,6},{4,0},{6,2},{1,5},{3,7},{5,1},{7,3},{8,12},{10,14},{12... | collective-permute-start | bytes 786440 | tf_op jit(solution)/shard_map/ppermute | solution.py:290
  856.7 1.3 copy-start.11
Sparse Core Ops, SparseCore 0:
  243.5 54.6 all-gather.3
  411.1 53.1 all-gather.5
  712.9 106.3 all-gather.7

commit v4 on v3

--- a/solution.py
+++ b/solution.py
@@ -45,7 +45,12 @@
     return jnp.max(sums, axis=0, keepdims=True)
 
 
-def attend(queries, key_parts, value_parts, ids, lengths, j, nj, start, stride, count):
+def key_bound(key_parts):
+    squares = [jnp.max(jnp.sum(jnp.square(part.astype(F32)), axis=-1)) for part in key_parts]
+    return functools.reduce(jnp.maximum, squares)[None]
+
+
+def attend(queries, key_parts, value_parts, bound, ids, lengths, j, nj, start, stride, count):
     _, rows, width = queries.shape
     local, head = key_parts[0].shape[1:]
     cached = local - rows
@@ -65,15 +70,13 @@
     scale = math.log2(math.e) / math.sqrt(head)
     capacity = span + shards * cached + block
 
-    def kernel(meta_ref, len_ref, q_ref, *refs):
+    def kernel(meta_ref, len_ref, bound_ref, q_ref, *refs):
         key_refs, value_refs = refs[:parts], refs[parts : 2 * parts]
-        o_ref, staged, keys, values, stacked, acc, top, norms, counts, bounds, arrived = refs[2 * parts :]
+        o_ref, staged, keys, values, stacked, acc, top, counts, arrived = refs[2 * parts :]
         step = pl.program_id(0)
 
         @pl.when(step == 0)
         def _():
-            norms[...] = jnp.zeros_like(norms)
-
             index = lax.broadcasted_iota(jnp.int32, (slot, head), 0)
             copies = []
             for which, pieces in enumerate((key_refs, value_refs)):
@@ -94,19 +97,15 @@
             def put_shard(n, at):
                 shard = meta_ref[2 + n]
                 place = pl.ds(pl.multiple_of(shard * rows, rows), rows)
-                piece = staged[0, n, cached:, :]
-                keys[place, :] = piece
+                keys[place, :] = staged[0, n, cached:, :]
                 values[place, :head] = staged[1, n, cached:, :]
                 values[place, head:] = jnp.ones((rows, head), BF16)
-                norms[...] = jnp.maximum(norms[...], square_bound(piece))
                 for k in range(per_shard):
-                    piece = staged[0, n, k * slot : (k + 1) * slot, :]
                     size = len_ref[shard * per_shard + k]
                     place = pl.ds(pl.multiple_of(at, 16), slot)
-                    keys[place, :] = piece
+                    keys[place, :] = staged[0, n, k * slot : (k + 1) * slot, :]
                     values[place, :head] = staged[1, n, k * slot : (k + 1) * slot, :]
                     values[place, head:] = jnp.where(index < size, 1.0, 0.0).astype(BF16)
-                    norms[...] = jnp.maximum(norms[...], square_bound(piece))
                     at = at + (size + 15) // 16 * 16
                 return at
 
@@ -115,7 +114,6 @@
             keys[place, :] = jnp.broadcast_to(staged[0, 0, 0:1, :], (block, head))
             values[place, :] = jnp.zeros((block, pair), BF16)
             counts[0] = (end - span + block - 1) // block
-            bounds[0] = jnp.max(norms[...])
 
         for g in range(group):
             stacked[g * rows : (g + 1) * rows, :] = q_ref[0, :, g * head : (g + 1) * head]
@@ -124,7 +122,7 @@
         full = first_token // block
         total = full + counts[0]
         query_bound = jnp.max(square_bound(stacked[...]))
-        safe = query_bound * bounds[0] * (1.03 * scale * scale) <= bound_limit * bound_limit
+        safe = query_bound * bound_ref[0] * (1.03 * scale * scale) <= bound_limit * bound_limit
 
         def scores_of(at, part):
             raw = lax.dot_general(
@@ -209,6 +207,7 @@
         num_scalar_prefetch=2,
         grid=(count,),
         in_specs=[
+            pl.BlockSpec(memory_space=pltpu.SMEM),
             pl.BlockSpec((1, rows, width), lambda i, meta, size: (meta[1] + i * stride, 0, 0)),
         ]
         + [pl.BlockSpec(memory_space=pl.ANY)] * (2 * parts),
@@ -220,9 +219,7 @@
             pltpu.VMEM((stack, head), BF16),
             pltpu.VMEM((stack, pair), F32),
             pltpu.VMEM((stack, head), F32),
-            pltpu.VMEM((1, head), F32),
             pltpu.SMEM((1,), jnp.int32),
-            pltpu.SMEM((1,), F32),
             pltpu.SemaphoreType.DMA((2 * parts,)),
         ],
     )
@@ -232,10 +229,10 @@
         out_shape=jax.ShapeDtypeStruct((count, rows, width), BF16),
         compiler_params=pltpu.CompilerParams(vmem_limit_bytes=60 << 20),
         name="attend",
-    )(meta, lengths, queries, *key_parts, *value_parts)
-
-
-def project(rotated, key_parts, value_parts, ids, lengths, out_weight, j, nz, nj, nt):
+    )(meta, lengths, bound, queries, *key_parts, *value_parts)
+
+
+def project(rotated, key_parts, value_parts, bound, ids, lengths, out_weight, j, nz, nj, nt):
     groups = nz // nt
     rows, columns = rotated.shape[1], out_weight.shape[1]
     half = out_weight.shape[0] // 2
@@ -248,7 +245,7 @@
         calls = [(owner, 1) for owner in reversed(range(nt))] if g < groups - 1 else [(0, nt)]
         for owner, count in calls:
             first = owner * groups + g
-            part = attend(rotated, key_parts, value_parts, ids, lengths, j, nj, first, groups, count)
+            part = attend(rotated, key_parts, value_parts, bound, ids, lengths, j, nj, first, groups, count)
             pieces.append(lax.all_gather(part, "z", axis=2, tiled=True))
     across = (move(1, far[:half]), move(2, near[half:]))
     weights = [(out_weight,), (near,), (far,), across]
@@ -323,11 +320,11 @@
     if split:
         ids = jnp.concatenate([every + j, every + (j ^ 1), every + (j ^ 2), every + (j ^ 3)]).astype(jnp.int32)
         key_parts, value_parts = spread(keys), spread(values)
-        return project(rotated, key_parts, value_parts, ids, lengths, out_weight, j, nz, nj, nt)
+        return project(rotated, key_parts, value_parts, key_bound(key_parts), ids, lengths, out_weight, j, nz, nj, nt)
     ids = (jnp.arange(nj, dtype=jnp.int32)[:, None] + every[None, :]).reshape(-1)
     key_parts = [lax.all_gather(keys, "j", axis=0, tiled=True)]
     value_parts = [lax.all_gather(values, "j", axis=0, tiled=True)]
-    attention = attend(rotated, key_parts, value_parts, ids, lengths, j, nj, 0, 1, nz)
+    attention = attend(rotated, key_parts, value_parts, key_bound(key_parts), ids, lengths, j, nj, 0, 1, nz)
     wide = attention.reshape(nz * rows, -1)
     wide = lax.all_gather(wide, ("z", "j"), axis=0, tiled=True)
     projected = jnp.dot(wide, out_weight, preferred_element_type=F32).astype(BF16)

time: 866 us -> 854 us (0.986)
  waiting for transfers between devices: 90.9 us -> 78.4 us
  Pallas kernels: 576 us -> 565 us
    ppermute x18, waiting for transfers between devices: 81.9 us -> 69.3 us  [move(): return lax.ppermute(array, 'j', [(i, i ^ r) for i in range(4)])]
    pallas_call x3, Pallas kernels: 576 us -> 565 us  [attend(): pl.pallas_call(kernel, grid_spec=grid_spec, out_shape=jax.ShapeDtypeStruc...]
  transfers between devices with their start and end apart: 31 -> 31, of which waited for: 11 -> 10; matrix products, arithmetic and copies ran while one was open for 8% -> 10% of each run, Pallas kernels for 53% -> 53%
where the time goes in v4:
time: 854 us; the launch traced here: 853 us
  Pallas kernels  565 us (66%)
  waiting for transfers between devices  78.4 us (9%)
  starting transfers between devices  65.6 us (8%)
  matrix products  53 us (6%)
  local copies, waits for them, and re-layouts  31.6 us (4%)
  blocking collectives  26.2 us (3%)
  between operations  17.7 us (2%)
  other arithmetic  15.1 us (2%)
    pallas_call x3, Pallas kernels, attend(): pl.pallas_call(kernel, grid_spec=grid_spec, out_shape=jax.ShapeDtypeStruc...  565 us
    ppermute x18, waiting for transfers between devices, move(): return lax.ppermute(array, 'j', [(i, i ^ r) for i in range(4)])  69.3 us
    ppermute x18, starting transfers between devices, move(): return lax.ppermute(array, 'j', [(i, i ^ r) for i in range(4)])  56.3 us
    dot_general x9, matrix products, times(): jnp.einsum('ctk,kn->ctn', left, weights[r][0], preferred_element_type=F32)  37.8 us
    all_to_all x1, blocking collectives, body(): keys = lax.all_to_all(keys, 'z', 0, 0, tiled=True)  26.2 us
  transfers between devices with their start and end apart: 31, of which 10 were waited for; matrix products, arithmetic and copies ran while one was open for 10% of the time, Pallas kernels for 53%

profile of v4, /device:TPU:0, one launch (start us, length us, event | category | flops | bytes accessed | tf_op | source)
XLA Modules:
  0.0 852.6 jit_solution(12035627700758035381)
XLA Ops:
  6.6 2.6 reshape.140
  14.7 26.2 %all_to_all.15.refs_0_ = bf16[4,768,128]{2,1,0:T(8,128)(2,1)S(1)} all-to-all(bf16[4,768,128]{2,1,0:T(8,128)(2,1)S(1)} %get-tuple-element.37), channel_id=1, replica_groups=mesh['z'=4,'j'=4,'tp'=2] {'z'}, dimensions={0} | all-to-all | bytes 1572864 | tf_op jit(solution)/shard_map/all_to_all | solution.py:314
  41.0 3.5 all-to-all-start.1
  44.5 4.3 copy.33
  48.8 2.9 subtract_convert_fusion
  53.2 4.0 copy.34
  57.1 6.6 all-to-all-done.1.refs_5_
  64.6 3.6 all-to-all-start.2
  68.3 1.6 collective-permute-start.1
  73.0 15.9 %collective-permute-done.1.refs_2_ = bf16[4,768,128]{2,1,0:T(8,128)(2,1)} collective-permute-done((bf16[4,768,128]{2,1,0:T(8,128)(2,1)S(1)}, bf16[4,768,128]{2,1,0:T(8,128)(2,1)}, u32[]{:S(2)}, u32[]{:S(2)}) %collective-permute-start.1) | collective-permute-done | bytes 786464 | tf_op jit(solution)/shard_map/ppermute | solution.py:287
  88.9 1.8 slice.89
  93.3 1.8 slice.90
  96.5 1.6 multiply_reduce_fusion
  98.8 6.9 collective-permute-done.5.refs_7_
  105.7 1.8 slice.93
  109.0 1.8 slice.94
  112.3 1.6 multiply_reduce_fusion.1
  119.7 2.1 collective-permute-done.6.refs_8_
  123.3 115.6 %attend.3 = bf16[1,256,1024]{2,1,0:T(8,128)(2,1)} custom-call(s32[18]{0:T(128)} %concatenate.38.meta_ref, s32[32]{0:T(128)} %len_ref.5, f32[1]{0:T(128)} %bitcast.8.bound_ref, bf16[4,256,1024]{2,1,0:T(8,128)(2,1)} %copy-done, bf16[4,768,128]{2,1,0:T(8,128)(2,1)} %copy-done.1, bf16[4,768,128]{2,1,0:T(8,128)(2,1)} %collective-permute-done.refs_1_, ...), custom_call_target="tpu_custom_call" | custom-call | tf_op jit(solution)/shard_map/attend/pallas_call | solution.py:226
  239.0 9.6 %collective-permute-start.12 = (bf16[4096,512]{1,0:T(8,128)(2,1)}, bf16[4096,512]{1,0:T(8,128)(2,1)}, u32[]{:S(2)}, u32[]{:S(2)}) collective-permute-start(bf16[4096,512]{1,0:T(8,128)(2,1)} %param.9), channel_id=1, source_target_pairs={{0,4},{2,6},{4,0},{6,2},{1,5},{3,7},{5,1},{7,3},{8,12},{10,14},{12... | collective-permute-start | bytes 12582920 | tf_op jit(solution)/shard_map/ppermute | solution.py:287
  250.7 152.0 %attend.4 = bf16[1,256,1024]{2,1,0:T(8,128)(2,1)} custom-call(s32[18]{0:T(128)} %concatenate.42.meta_ref, s32[32]{0:T(128)} %len_ref.5, f32[1]{0:T(128)} %bitcast.8.bound_ref, bf16[4,256,1024]{2,1,0:T(8,128)(2,1)} %copy-done, bf16[4,768,128]{2,1,0:T(8,128)(2,1)} %copy-done.1, bf16[4,768,128]{2,1,0:T(8,128)(2,1)} %collective-permute-done.refs_1_, ...), custom_call_target="tpu_custom_call" | custom-call | tf_op jit(solution)/shard_map/attend/pallas_call | solution.py:226
  403.5 297.2 %attend.5 = bf16[2,256,1024]{2,1,0:T(8,128)(2,1)} custom-call(s32[18]{0:T(128)} %concatenate.47.meta_ref, s32[32]{0:T(128)} %len_ref.5, f32[1]{0:T(128)} %bitcast.8.bound_ref, bf16[4,256,1024]{2,1,0:T(8,128)(2,1)} %copy-done, bf16[4,768,128]{2,1,0:T(8,128)(2,1)} %copy-done.1, bf16[4,768,128]{2,1,0:T(8,128)(2,1)} %collective-permute-done.refs_1_, ...), custom_call_target="tpu_custom_call" | custom-call | tf_op jit(solution)/shard_map/attend/pallas_call | solution.py:226
  700.8 1.7 slice.96
  703.0 3.0 slice.98
  706.1 27.1 %collective-permute-start.16 = (bf16[2048,512]{1,0:T(8,128)(2,1)}, bf16[2048,512]{1,0:T(8,128)(2,1)}, u32[]{:S(2)}, u32[]{:S(2)}) collective-permute-start(bf16[2048,512]{1,0:T(8,128)(2,1)} %slice.98), channel_id=1, source_target_pairs={{0,4},{2,6},{4,0},{6,2},{1,5},{3,7},{5,1},{7,3},{8,12},{10,14},{12... | collective-permute-start | bytes 6291464 | tf_op jit(solution)/shard_map/ppermute | solution.py:287
  733.2 4.6 fusion.31
  737.8 4.2 fusion.40
  742.2 3.6 fusion.46
  745.9 3.5 fusion.37
  749.9 3.5 fusion.43
  753.4 3.5 fusion.34
  757.5 22.1 %collective-permute-done.16 = bf16[2048,512]{1,0:T(8,128)(2,1)} collective-permute-done((bf16[2048,512]{1,0:T(8,128)(2,1)}, bf16[2048,512]{1,0:T(8,128)(2,1)}, u32[]{:S(2)}, u32[]{:S(2)}) %collective-permute-start.16) | collective-permute-done | bytes 2097184 | tf_op jit(solution)/shard_map/ppermute | solution.py:287
  779.7 2.3 fusion.49
  782.0 2.3 fusion.29
  784.3 2.3 fusion.50
  786.7 2.3 fusion.30
  791.4 2.2 collective-permute-start.18
  793.6 5.0 collective-permute-done.11
  798.7 6.2 collective-permute-done.18
  804.9 2.3 all-gather.8.cloned.1.call-done
  807.3 5.9 fusion
  813.3 4.5 fusion.4
  818.5 3.1 fusion.6
  821.5 2.8 fusion.24
  824.5 4.5 fusion.2
  829.7 2.4 collective-permute-start.20
  833.6 6.3 collective-permute-done.20
  839.9 4.7 collective-permute-done.22
  (129 shorter events, 33.5 us)
Async XLA Ops:
  6.5 2.7 copy-start.5
  6.6 4.0 copy-start.9
  6.6 5.4 copy-start.8
  41.0 51.2 %copy-start.1 = (bf16[4,768,128]{2,1,0:T(8,128)(2,1)}, bf16[4,768,128]{2,1,0:T(8,128)(2,1)S(1)}, u32[]{:S(2)}) copy-start(bf16[4,768,128]{2,1,0:T(8,128)(2,1)S(1)} %all_to_all.15.refs_0_) | copy-start | bytes 2359300
  41.0 22.8 %all-to-all-start.1 = ((bf16[4,768,128]{2,1,0:T(8,128)(2,1)}), bf16[4,768,128]{2,1,0:T(8,128)(2,1)S(1)}, u32[]{:S(2)}, u32[]{:S(2)}) async-start(bf16[4,768,128]{2,1,0:T(8,128)(2,1)} %get-tuple-element.21), calls=%async_computation.1 | async-start | bytes 1572864 | tf_op jit(solution)/shard_map/all_to_all | solution.py:316
  63.8 0.9 copy-start.2
  64.6 57.2 %all-to-all-start.2 = ((bf16[4,256,1024]{2,1,0:T(8,128)(2,1)}), bf16[4,256,1024]{2,1,0:T(8,128)(2,1)S(1)}, u32[]{:S(2)}, u32[]{:S(2)}) async-start(bf16[4,256,1024]{2,1,0:T(8,128)(2,1)} %bitcast.190), calls=%async_computation.2 | async-start | bytes 4194304 | tf_op jit(solution)/shard_map/all_to_all | solution.py:318
  68.2 665.0 %all-gather.4.cloned.1.call-start = ((), (), s32[]{:S(2)}) async-start(), calls=%async_computation.3 | async-start | bytes 2621440 | tf_op jit(solution)/shard_map/all_gather | solution.py:249
  68.3 20.6 %collective-permute-start.1 = (bf16[4,768,128]{2,1,0:T(8,128)(2,1)S(1)}, bf16[4,768,128]{2,1,0:T(8,128)(2,1)}, u32[]{:S(2)}, u32[]{:S(2)}) collective-permute-start(bf16[4,768,128]{2,1,0:T(8,128)(2,1)S(1)} %all_to_all.15.refs_0_), channel_id=1, source_target_pairs={{0,4},{2,6},{4,0},{6,2},{1,5},{3,7},{5,1},{7,3},{8,12},{10,14},{12... | collective-permute-start | bytes 2359304 | tf_op jit(solution)/shard_map/ppermute | solution.py:287
  69.9 23.4 %collective-permute-start = (bf16[4,768,128]{2,1,0:T(8,128)(2,1)S(1)}, bf16[4,768,128]{2,1,0:T(8,128)(2,1)}, u32[]{:S(2)}, u32[]{:S(2)}) collective-permute-start(bf16[4,768,128]{2,1,0:T(8,128)(2,1)S(1)} %all_to_all.15.refs_0_), channel_id=1, source_target_pairs={{0,2},{2,0},{4,6},{6,4},{1,3},{3,1},{5,7},{7,5},{8,10},{10,8},{12,... | collective-permute-start | bytes 2359304 | tf_op jit(solution)/shard_map/ppermute | solution.py:287
  71.4 34.4 %collective-permute-start.5 = (bf16[4,768,128]{2,1,0:T(8,128)(2,1)}, bf16[4,768,128]{2,1,0:T(8,128)(2,1)}, u32[]{:S(2)}, u32[]{:S(2)}) collective-permute-start(bf16[4,768,128]{2,1,0:T(8,128)(2,1)} %copy-done.2), channel_id=1, source_target_pairs={{0,4},{2,6},{4,0},{6,2},{1,5},{3,7},{5,1},{7,3},{8,12},{10,14},{12... | collective-permute-start | bytes 2359304 | tf_op jit(solution)/shard_map/ppermute | solution.py:287
  71.9 37.1 %collective-permute-start.4 = (bf16[4,768,128]{2,1,0:T(8,128)(2,1)}, bf16[4,768,128]{2,1,0:T(8,128)(2,1)}, u32[]{:S(2)}, u32[]{:S(2)}) collective-permute-start(bf16[4,768,128]{2,1,0:T(8,128)(2,1)} %copy-done.2), channel_id=1, source_target_pairs={{0,2},{2,0},{4,6},{6,4},{1,3},{3,1},{5,7},{7,5},{8,10},{10,8},{12,... | collective-permute-start | bytes 2359304 | tf_op jit(solution)/shard_map/ppermute | solution.py:287
  90.6 25.9 %collective-permute-start.2 = (bf16[2,768,128]{2,1,0:T(8,128)(2,1)}, bf16[2,768,128]{2,1,0:T(8,128)(2,1)S(1)}, u32[]{:S(2)}, u32[]{:S(2)}) collective-permute-start(bf16[2,768,128]{2,1,0:T(8,128)(2,1)} %slice.89), channel_id=1, source_target_pairs={{0,2},{2,0},{4,6},{6,4},{1,3},{3,1},{5,7},{7,5},{8,10},{10,8},{12,... | collective-permute-start | bytes 1179656 | tf_op jit(solution)/shard_map/ppermute | solution.py:287
  95.0 22.4 %collective-permute-start.3 = (bf16[2,768,128]{2,1,0:T(8,128)(2,1)}, bf16[2,768,128]{2,1,0:T(8,128)(2,1)S(1)}, u32[]{:S(2)}, u32[]{:S(2)}) collective-permute-start(bf16[2,768,128]{2,1,0:T(8,128)(2,1)} %slice.90), channel_id=1, source_target_pairs={{0,4},{2,6},{4,0},{6,2},{1,5},{3,7},{5,1},{7,3},{8,12},{10,14},{12... | collective-permute-start | bytes 1179656 | tf_op jit(solution)/shard_map/ppermute | solution.py:287
  107.5 14.3 %collective-permute-start.6 = (bf16[2,768,128]{2,1,0:T(8,128)(2,1)}, bf16[2,768,128]{2,1,0:T(8,128)(2,1)S(1)}, u32[]{:S(2)}, u32[]{:S(2)}) collective-permute-start(bf16[2,768,128]{2,1,0:T(8,128)(2,1)} %slice.93), channel_id=1, source_target_pairs={{0,2},{2,0},{4,6},{6,4},{1,3},{3,1},{5,7},{7,5},{8,10},{10,8},{12,... | collective-permute-start | bytes 1179656 | tf_op jit(solution)/shard_map/ppermute | solution.py:287
  110.8 11.0 %collective-permute-start.7 = (bf16[2,768,128]{2,1,0:T(8,128)(2,1)}, bf16[2,768,128]{2,1,0:T(8,128)(2,1)}, u32[]{:S(2)}, u32[]{:S(2)}) collective-permute-start(bf16[2,768,128]{2,1,0:T(8,128)(2,1)} %slice.94), channel_id=1, source_target_pairs={{0,4},{2,6},{4,0},{6,2},{1,5},{3,7},{5,1},{7,3},{8,12},{10,14},{12... | collective-permute-start | bytes 1179656 | tf_op jit(solution)/shard_map/ppermute | solution.py:287
  116.5 5.4 copy-start.3
  117.5 4.5 copy-start.4
  121.9 0.8 copy-start.6
  121.9 1.4 copy-start
  239.0 498.8 %all-gather.6.cloned.1.call-start = ((), (), s32[]{:S(2)}) async-start(), calls=%async_computation.4 | async-start | bytes 2621440 | tf_op jit(solution)/shard_map/all_gather | solution.py:249
  239.0 461.8 %collective-permute-start.12 = (bf16[4096,512]{1,0:T(8,128)(2,1)}, bf16[4096,512]{1,0:T(8,128)(2,1)}, u32[]{:S(2)}, u32[]{:S(2)}) collective-permute-start(bf16[4096,512]{1,0:T(8,128)(2,1)} %param.9), channel_id=1, source_target_pairs={{0,4},{2,6},{4,0},{6,2},{1,5},{3,7},{5,1},{7,3},{8,12},{10,14},{12... | collective-permute-start | bytes 12582920 | tf_op jit(solution)/shard_map/ppermute | solution.py:287
  248.6 454.4 %collective-permute-start.9 = (bf16[4096,512]{1,0:T(8,128)(2,1)}, bf16[4096,512]{1,0:T(8,128)(2,1)}, u32[]{:S(2)}, u32[]{:S(2)}) collective-permute-start(bf16[4096,512]{1,0:T(8,128)(2,1)} %param.9), channel_id=1, source_target_pairs={{0,2},{2,0},{4,6},{6,4},{1,3},{3,1},{5,7},{7,5},{8,10},{10,8},{12,... | collective-permute-start | bytes 12582920 | tf_op jit(solution)/shard_map/ppermute | solution.py:287
  402.8 404.4 %all-gather.8.cloned.1.call-start = ((), (), s32[]{:S(2)}) async-start(), calls=%async_computation.5 | async-start | bytes 5242880 | tf_op jit(solution)/shard_map/all_gather | solution.py:249
  702.6 79.4 %collective-permute-start.15 = (bf16[2048,512]{1,0:T(8,128)(2,1)S(1)}, bf16[2048,512]{1,0:T(8,128)(2,1)}, u32[]{:S(2)}, u32[]{:S(2)}) collective-permute-start(bf16[2048,512]{1,0:T(8,128)(2,1)S(1)} %slice.96), channel_id=1, source_target_pairs={{0,2},{2,0},{4,6},{6,4},{1,3},{3,1},{5,7},{7,5},{8,10},{10,8},{12,... | collective-permute-start | bytes 6291464 | tf_op jit(solution)/shard_map/ppermute | solution.py:287
  706.1 73.6 %collective-permute-start.16 = (bf16[2048,512]{1,0:T(8,128)(2,1)}, bf16[2048,512]{1,0:T(8,128)(2,1)}, u32[]{:S(2)}, u32[]{:S(2)}) collective-permute-start(bf16[2048,512]{1,0:T(8,128)(2,1)} %slice.98), channel_id=1, source_target_pairs={{0,4},{2,6},{4,0},{6,2},{1,5},{3,7},{5,1},{7,3},{8,12},{10,14},{12... | collective-permute-start | bytes 6291464 | tf_op jit(solution)/shard_map/ppermute | solution.py:287
  737.8 4.4 copy-start.12
  742.1 3.7 copy-start.11
  742.1 48.8 %collective-permute-start.8 = (bf16[256,512]{1,0:T(8,128)(2,1)S(1)}, bf16[256,512]{1,0:T(8,128)(2,1)S(1)}, u32[]{:S(2)}, u32[]{:S(2)}) collective-permute-start(bf16[256,512]{1,0:T(8,128)(2,1)S(1)} %fusion.87), channel_id=1, source_target_pairs={{0,1},{1,0},{2,3},{3,2},{4,5},{5,4},{6,7},{7,6},{8,9},{9,8},{10,11... | collective-permute-start | bytes 786440 | tf_op jit(solution)/shard_map/ppermute | solution.py:271
  749.5 7.8 collective-permute-start.13
  757.0 32.2 %collective-permute-start.10 = (bf16[256,512]{1,0:T(8,128)(2,1)S(1)}, bf16[256,512]{1,0:T(8,128)(2,1)S(1)}, u32[]{:S(2)}, u32[]{:S(2)}) collective-permute-start(bf16[256,512]{1,0:T(8,128)(2,1)S(1)} %fusion.88), channel_id=1, source_target_pairs={{0,1},{1,0},{2,3},{3,2},{4,5},{5,4},{6,7},{7,6},{8,9},{9,8},{10,11... | collective-permute-start | bytes 786440 | tf_op jit(solution)/shard_map/ppermute | solution.py:271
  757.4 41.2 %collective-permute-start.14 = (bf16[256,512]{1,0:T(8,128)(2,1)S(1)}, bf16[256,512]{1,0:T(8,128)(2,1)S(1)}, u32[]{:S(2)}, u32[]{:S(2)}) collective-permute-start(bf16[256,512]{1,0:T(8,128)(2,1)S(1)} %fusion.62), channel_id=1, source_target_pairs={{0,4},{2,6},{4,0},{6,2},{1,5},{3,7},{5,1},{7,3},{8,12},{10,14},{12... | collective-permute-start | bytes 786440 | tf_op jit(solution)/shard_map/ppermute | solution.py:287
  789.1 2.1 collective-permute-start.17
  789.3 9.2 %collective-permute-start.11 = (bf16[256,512]{1,0:T(8,128)(2,1)S(1)}, bf16[256,512]{1,0:T(8,128)(2,1)S(1)}, u32[]{:S(2)}, u32[]{:S(2)}) collective-permute-start(bf16[256,512]{1,0:T(8,128)(2,1)S(1)} %fusion.68), channel_id=1, source_target_pairs={{0,2},{2,0},{4,6},{6,4},{1,3},{3,1},{5,7},{7,5},{8,10},{10,8},{12,... | collective-permute-start | bytes 786440 | tf_op jit(solution)/shard_map/ppermute | solution.py:287
  791.4 13.5 %collective-permute-start.18 = (bf16[256,512]{1,0:T(8,128)(2,1)S(1)}, bf16[256,512]{1,0:T(8,128)(2,1)S(1)}, u32[]{:S(2)}, u32[]{:S(2)}) collective-permute-start(bf16[256,512]{1,0:T(8,128)(2,1)S(1)} %fusion.56), channel_id=1, source_target_pairs={{0,6},{2,4},{4,2},{6,0},{1,7},{3,5},{5,3},{7,1},{8,14},{10,12},{12... | collective-permute-start | bytes 786440 | tf_op jit(solution)/shard_map/ppermute | solution.py:287
  807.3 6.1 copy-start.10
  813.2 31.4 %collective-permute-start.25 = (bf16[256,512]{1,0:T(8,128)(2,1)S(1)}, bf16[256,512]{1,0:T(8,128)(2,1)S(1)}, u32[]{:S(2)}, u32[]{:S(2)}) collective-permute-start(bf16[256,512]{1,0:T(8,128)(2,1)S(1)} %fusion.82), channel_id=1, source_target_pairs={{0,1},{1,0},{2,3},{3,2},{4,5},{5,4},{6,7},{7,6},{8,9},{9,8},{10,11... | collective-permute-start | bytes 786440 | tf_op jit(solution)/shard_map/ppermute | solution.py:271
  817.9 14.3 %collective-permute-start.21 = (bf16[256,512]{1,0:T(8,128)(2,1)S(1)}, bf16[256,512]{1,0:T(8,128)(2,1)S(1)}, u32[]{:S(2)}, u32[]{:S(2)}) collective-permute-start(bf16[256,512]{1,0:T(8,128)(2,1)S(1)} %fusion.80), channel_id=1, source_target_pairs={{0,1},{1,0},{2,3},{3,2},{4,5},{5,4},{6,7},{7,6},{8,9},{9,8},{10,11... | collective-permute-start | bytes 786440 | tf_op jit(solution)/shard_map/ppermute | solution.py:271
  824.4 5.2 collective-permute-start.19
  829.1 3.8 collective-permute-start.23
  829.7 10.2 %collective-permute-start.20 = (bf16[256,512]{1,0:T(8,128)(2,1)S(1)}, bf16[256,512]{1,0:T(8,128)(2,1)S(1)}, u32[]{:S(2)}, u32[]{:S(2)}) collective-permute-start(bf16[256,512]{1,0:T(8,128)(2,1)S(1)} %fusion.78), channel_id=1, source_target_pairs={{0,6},{2,4},{4,2},{6,0},{1,7},{3,5},{5,3},{7,1},{8,14},{10,12},{12... | collective-permute-start | bytes 786440 | tf_op jit(solution)/shard_map/ppermute | solution.py:287
  832.2 12.3 %collective-permute-start.22 = (bf16[256,512]{1,0:T(8,128)(2,1)S(1)}, bf16[256,512]{1,0:T(8,128)(2,1)S(1)}, u32[]{:S(2)}, u32[]{:S(2)}) collective-permute-start(bf16[256,512]{1,0:T(8,128)(2,1)S(1)} %fusion.77), channel_id=1, source_target_pairs={{0,2},{2,0},{4,6},{6,4},{1,3},{3,1},{5,7},{7,5},{8,10},{10,8},{12,... | collective-permute-start | bytes 786440 | tf_op jit(solution)/shard_map/ppermute | solution.py:287
  832.9 11.7 %collective-permute-start.24 = (bf16[256,512]{1,0:T(8,128)(2,1)S(1)}, bf16[256,512]{1,0:T(8,128)(2,1)S(1)}, u32[]{:S(2)}, u32[]{:S(2)}) collective-permute-start(bf16[256,512]{1,0:T(8,128)(2,1)S(1)} %fusion.76), channel_id=1, source_target_pairs={{0,4},{2,6},{4,0},{6,2},{1,5},{3,7},{5,1},{7,3},{8,12},{10,14},{12... | collective-permute-start | bytes 786440 | tf_op jit(solution)/shard_map/ppermute | solution.py:287
  844.7 1.3 copy-start.7
Sparse Core Ops, SparseCore 0:
  239.1 54.8 all-gather.3
  402.9 53.2 all-gather.5
  700.9 106.3 all-gather.7
